TPU v7x, 32 devices: a whole 2x2x4 slice. The times are simulated.
32 devices in a mesh: row: 4 (over y, core), col: 8 (over z, x).
Axes of the slice: x: 2, y: 2, z: 4, core: 2. Of those that a mesh axis runs over, the one named last changes fastest.
Arguments:
- objects: float32 [2, 2, 1024, 2048], P(None, None, 'row', 'col'), may hold values from -5 to 5
- probe: float32 [2, 256, 256], replicated, may hold values from -6 to 6
- prev_partial: float32 [4, 8, 2, 256, 256], P('row', 'col'), may hold values from -6 to 6
- offsets: int32 [4, 8, 1, 2], P('row', 'col'), may hold values from 0 to 128
- counts: int32 [4, 8], P('row', 'col'), may hold values from 0 to 1
- amplitudes: float32 [4, 8, 1, 256, 256], P('row', 'col'), may hold values from 1 to 2.5
Outputs:
- new_objects: float32 [2, 2, 1024, 2048], P(None, None, 'row', 'col')
- new_probe: float32 [2, 256, 256], replicated
- new_partial: float32 [4, 8, 2, 256, 256], P('row', 'col')
All inputs are finite; a program needn't handle non-finite values.
Results may differ from a plain program's by a relative error of at most 0.0003.
Values sent between devices are 32-bit elements; how exact they have to be, the bound alone decides.
A program may use at most 64 MiB of HBM per device.

v0:
```python
import functools
import math

import jax
import jax.numpy as jnp
import numpy as np
from jax import lax
from jax.experimental import pallas as pl
from jax.experimental.pallas import tpu as pltpu
from jax.sharding import PartitionSpec as P

HALO = 64
OBJ_RATE = 0.1
PROBE_RATE = 0.3
MESH = pl.DeviceIdType.MESH


def split(value):
    high = value.astype(jnp.bfloat16)
    low = (value - high.astype(jnp.float32)).astype(jnp.bfloat16)
    return high, low


def operator_table(n):
    index = np.arange(n)
    angle = 2.0 * np.pi * (np.outer(index, index) % n) / n
    dft = np.exp(-1j * angle) / np.sqrt(n)
    freq = np.where(index < n // 2, index, index - n).astype(np.float64)
    phase = np.exp(1j * np.pi * freq * freq / (4.0 * n))
    prop = np.conj(dft) @ (phase[:, None] * dft)
    tables = []
    for mat in (dft, prop):
        for part in (mat.real, mat.imag, -mat.imag):
            part = part.astype(np.float32)
            high = part.astype(jnp.bfloat16)
            low = (part - high.astype(np.float32)).astype(jnp.bfloat16)
            tables += [high, low]
    return np.stack(tables).reshape(2, 3, 2, n, n)


def dot(left, right):
    return jnp.dot(left, right, preferred_element_type=jnp.float32)


def cat(parts, axis):
    return jnp.concatenate(parts, axis=axis)


def sandwich(xr, xi, table, which, conj):
    re, im, neg = table.at[which, 0], table.at[which, 1], table.at[which, 2]
    if conj:
        im, neg = neg, im
    rh, rl, ih, il, nh, nl = (p[k] for p in (re, im, neg) for k in (0, 1))
    xrh, xrl = split(xr)
    xih, xil = split(xi)
    left = cat([xrh, xih, xrl, xil, xrh, xih], 1)
    tr = dot(left, cat([rh, nh, rh, nh, rl, nl], 0))
    ti = dot(left, cat([ih, rh, ih, rh, il, rl], 0))
    trh, trl = split(tr)
    tih, til = split(ti)
    right = cat([trh, tih, trl, til, trh, tih], 0)
    yr = dot(cat([rh, nh, rh, nh, rl, nl], 1), right)
    yi = dot(cat([ih, rh, ih, rh, il, rl], 1), right)
    return yr, yi


def kernel(
    rows, cols, offs, count, obj_hbm, prev_hbm, probe_hbm, probe_k_hbm, amp_hbm, table_hbm,
    out_obj, out_probe, out_part,
    obj, prev, probe, probe_piece, amp, table,
    my_off, off,
    ns_in, strip_mid, strip_edge, fold_far, far_mid, far_edge, msg_mid, msg_edge, got_mid, got_edge, z,
    gmsg_mid, gmsg_edge, gs_mid, gs_edge, acc_mid, acc_edge, ns_out, ns_back, new_mid, new_edge, part,
    buf1, sum1, buf2, newp,
    local_sem, out_sem, off_send, off_recv, ns_send, ns_recv, far_send, far_recv, msg_send, msg_recv,
    row_send, row_recv, col_send, col_recv, known,
):
    tile = obj.shape[2]
    mid_rows = tile - 2 * HALO
    wide = 2 * HALO
    row, col = lax.axis_index("row"), lax.axis_index("col")
    odd = lax.rem(col, 2)
    step = 1 - 2 * odd
    near = 1 - odd
    far = odd
    partner, other = col + step, col - step
    ahead, behind = col + 2 * step, col - 2 * step
    has_other = (other >= 0) & (other < cols)
    has_ahead = (ahead >= 0) & (ahead < cols)
    has_behind = (behind >= 0) & (behind < cols)
    has_north, has_south = row > 0, row < rows - 1
    always = row >= 0

    fetches = [
        pltpu.make_async_copy(src, dst, local_sem.at[k])
        for k, (src, dst) in enumerate(
            ((obj_hbm.at[0], obj.at[0]), (obj_hbm.at[1], obj.at[1]), (prev_hbm, prev),
             (probe_hbm, probe), (probe_k_hbm.at[row, col], probe_piece),
             (table_hbm, table), (amp_hbm, amp))
        )
    ]
    for fetch in fetches:
        fetch.start()

    barrier = pltpu.get_barrier_semaphore()

    def greet(sem, r, c):
        pl.semaphore_signal(sem, inc=1, device_id=(r, c), device_id_type=MESH)

    def flip(value, bit):
        return value + bit * (1 - 2 * lax.rem(value // bit, 2))

    bits = [1 << k for k in range(cols.bit_length() - 1)]
    expected = 0
    for t in range(1, rows):
        greet(barrier, lax.rem(row + t, rows), col)
        expected = expected + 1
    for ok, c in ((always, partner), (has_other, other), (has_ahead, ahead), (has_behind, behind)):
        @pl.when(ok)
        def _():
            greet(barrier, row, c)
        expected = expected + ok.astype(jnp.int32)
    for bit in bits[2:]:
        greet(barrier, row, flip(col, bit))
        expected = expected + 1

    top, left = offs[0], offs[1]
    my_off[0] = jnp.zeros((8, wide), jnp.int32) + top
    my_off[1] = jnp.zeros((8, wide), jnp.int32) + left

    lane = lax.broadcasted_iota(jnp.int32, (1, wide), 1)
    first = lane < HALO
    lane64 = jnp.where(first, lane, lane - HALO)
    line = lax.broadcasted_iota(jnp.int32, (wide, 1), 0)

    def swap(value):
        return pltpu.roll(value, HALO, 1)

    def turned(index, corner):
        return (index < corner - HALO) | (index >= corner + HALO)

    def pack(ref, slot):
        re, im = ref
        if slot == 0:
            return jnp.where(first, re[:, :wide], swap(im[:, :wide]))
        return jnp.where(first, swap(re[:, tile - wide :]), im[:, tile - wide :])

    def ends(value):
        return cat([value[:HALO], value[tile - HALO :]], 0)

    for s in range(2):
        fetches[s].wait()
        for slot in range(2):
            value = pack((obj[s, 0], obj[s, 1]), slot)
            strip_mid[slot, s] = value[HALO : tile - HALO]
            strip_edge[slot, s] = ends(value)
    fetches[3].wait()
    turn_rows = lax.rem(top + tile - HALO, tile)
    turn_cols = lax.rem(left + tile - HALO, tile)
    for k in range(2):
        probe[k] = pltpu.roll(pltpu.roll(probe[k], turn_rows, 0), turn_cols, 1)

    @pl.when(jnp.logical_not(has_other))
    def _():
        off[far] = jnp.full((2, 8, wide), HALO, jnp.int32)

    for s in range(2):
        @pl.when(jnp.logical_not(has_south))
        def _():
            ns_in[s, :, :HALO, :] = jnp.zeros((2, HALO, tile), jnp.float32)
            ns_back[s, :, HALO:, :] = jnp.zeros((2, HALO, tile), jnp.float32)

        @pl.when(jnp.logical_not(has_north))
        def _():
            ns_in[s, :, HALO:, :] = jnp.zeros((2, HALO, tile), jnp.float32)
            ns_back[s, :, :HALO, :] = jnp.zeros((2, HALO, tile), jnp.float32)

        @pl.when(jnp.logical_not(has_ahead))
        def _():
            far_mid[s] = jnp.zeros((mid_rows, wide), jnp.float32)
            far_edge[s] = jnp.zeros((wide, wide), jnp.float32)

        @pl.when(jnp.logical_not(has_behind))
        def _():
            gs_mid[far, s] = jnp.zeros((mid_rows, wide), jnp.float32)
            gs_edge[far, s] = jnp.zeros((wide, wide), jnp.float32)

    class Link:
        def __init__(self, src, dst, send_sem, recv_sem, device, ok, inbound):
            self.copy = pltpu.make_async_remote_copy(
                src_ref=src, dst_ref=dst, send_sem=send_sem, recv_sem=recv_sem,
                device_id=device, device_id_type=MESH)
            self.ok, self.inbound = ok, inbound

        def start(self):
            @pl.when(self.ok)
            def _():
                self.copy.start()

        def arrive(self):
            @pl.when(self.inbound)
            def _():
                self.copy.wait_recv()

        def sent(self):
            @pl.when(self.ok)
            def _():
                self.copy.wait_send()

    up, down = slice(0, HALO), slice(HALO, wide)
    off_near = Link(my_off, off.at[1 - near], off_send.at[0], off_recv.at[0], (row, partner), always, always)
    off_far = Link(my_off, off.at[1 - far], off_send.at[1], off_recv.at[1], (row, other), has_other, has_other)

    def ns_links(phase, s):
        if phase == 0:
            src_up, src_down, dst = obj.at[s, :, up, :], obj.at[s, :, tile - HALO :, :], ns_in
            to_up, to_down = (row - 1, has_north, has_south), (row + 1, has_south, has_north)
        else:
            src_up, src_down, dst = ns_out.at[s, :, up, :], ns_out.at[s, :, down, :], ns_back
            to_up, to_down = (row + 1, has_south, has_north), (row - 1, has_north, has_south)
        return [
            Link(src, dst.at[s, :, span, :], ns_send.at[phase, s, k], ns_recv.at[phase, s, k], (to[0], col), to[1], to[2])
            for k, (src, span, to) in enumerate(((src_up, up, to_up), (src_down, down, to_down)))
        ]

    ns = [[ns_links(phase, s) for s in range(2)] for phase in range(2)]
    MID, EDGE = 0, 1
    far_link = [
        [
            Link(strip_mid.at[far, s], far_mid.at[s], far_send.at[0, s, 0], far_recv.at[0, s, 0], (row, behind), has_behind, has_ahead),
            Link(fold_far.at[s], far_edge.at[s], far_send.at[0, s, 1], far_recv.at[0, s, 1], (row, behind), has_behind, has_ahead),
        ]
        for s in range(2)
    ]
    msg_link = [
        [
            Link(msg_mid.at[s], got_mid.at[s], msg_send.at[0, s, 0], msg_recv.at[0, s, 0], (row, partner), always, always),
            Link(msg_edge.at[s], got_edge.at[s], msg_send.at[0, s, 1], msg_recv.at[0, s, 1], (row, partner), always, always),
        ]
        for s in range(2)
    ]
    gmsg_link = [
        [
            Link(gmsg_mid.at[s], gs_mid.at[1 - near, s], msg_send.at[1, s, 0], msg_recv.at[1, s, 0], (row, partner), always, always),
            Link(gmsg_edge.at[s], gs_edge.at[1 - near, s], msg_send.at[1, s, 1], msg_recv.at[1, s, 1], (row, partner), always, always),
        ]
        for s in range(2)
    ]
    pass_link = [
        [
            Link(gs_mid.at[near, s], gs_mid.at[far, s], far_send.at[1, s, 0], far_recv.at[1, s, 0], (row, ahead), has_ahead, has_behind),
            Link(gs_edge.at[near, s], gs_edge.at[far, s], far_send.at[1, s, 1], far_recv.at[1, s, 1], (row, ahead), has_ahead, has_behind),
        ]
        for s in range(2)
    ]

    def row_copies(stage):
        made = []
        for t in range(1, rows):
            peer = lax.rem(row + t, rows)
            if stage == 0:
                src, dst = prev.at[peer], buf1.at[t - 1]
            else:
                src, dst = newp.at[row], newp.at[row]
            made.append(pltpu.make_async_remote_copy(
                src_ref=src, dst_ref=dst, send_sem=row_send.at[stage, t - 1],
                recv_sem=row_recv.at[stage, t - 1], device_id=(peer, col), device_id_type=MESH))
        return made

    def col_copies(stage):
        made = []
        for t in range(1, cols):
            peer = lax.rem(col + t, cols)
            if stage == 0:
                src, dst = sum1.at[peer], buf2.at[t - 1]
            else:
                src, dst = newp.at[row, col], newp.at[row, col]
            made.append(pltpu.make_async_remote_copy(
                src_ref=src, dst_ref=dst, send_sem=col_send.at[stage, t - 1],
                recv_sem=col_recv.at[stage, t - 1], device_id=(row, peer), device_id_type=MESH))
        return made

    fetches[2].wait()
    pl.semaphore_wait(barrier, expected)

    off_near.start()
    off_far.start()
    for s in range(2):
        for link in ns[0][s]:
            link.start()
        far_link[s][MID].start()
    rs_rows = row_copies(0)
    for copy in rs_rows:
        copy.start()
    for bit in bits:
        greet(known.at[0], row, flip(col, bit))

    off_near.arrive()
    off_far.arrive()
    near_off, far_off = off[near], off[far]
    near_top, near_left = near_off[0, :1], near_off[1, :1]
    far_top = far_off[0, :1]
    take_own = jnp.where(near == 0, near_left - HALO, HALO - near_left) > 0

    def fold(s):
        for link in ns[0][s]:
            link.arrive()
        packs = [pack((ns_in[s, 0], ns_in[s, 1]), slot) for slot in range(2)]
        far_pack = jnp.where(far == 0, packs[0], packs[1])
        near_pack = jnp.where(near == 0, packs[0], packs[1])
        fold_far[s] = jnp.where(turned(line, far_top), far_pack, strip_edge[far, s])
        far_link[s][EDGE].start()
        msg_edge[s] = jnp.where(turned(line, near_top), near_pack, strip_edge[near, s])

    def forward_mid(s):
        far_link[s][MID].arrive()
        msg_mid[s] = jnp.where(take_own, strip_mid[near, s], far_mid[s])
        msg_link[s][MID].start()

    def forward_edge(s):
        far_link[s][EDGE].arrive()
        msg_edge[s] = jnp.where(take_own, msg_edge[s], far_edge[s])
        msg_link[s][EDGE].start()

    for s in range(2):
        fold(s)
        forward_mid(s)
    for s in range(2):
        forward_edge(s)

    for wait_round, bit in enumerate(bits[1:]):
        pl.semaphore_wait(known.at[wait_round], len(bits))
        if wait_round + 1 < len(bits) - 1:
            for again in bits:
                greet(known.at[wait_round + 1], row, flip(col, again))

    def assemble(s):
        from_east, from_west = lane < left - HALO, lane >= left + HALO

        def columns(base, strip):
            turned_strip = swap(strip)
            for k in range(2):
                re_like, im_like = (strip, turned_strip) if k == 0 else (turned_strip, strip)
                head = jnp.where(from_east, re_like, base[k][:, :wide])
                tail = jnp.where(from_west, im_like, base[k][:, tile - wide :])
                yield cat([head, base[k][:, wide : tile - wide], tail], 1) if tile > 2 * wide else cat([head, tail], 1)

        msg_link[s][MID].arrive()
        for k, value in enumerate(columns([obj[s, p, HALO : tile - HALO, :] for p in range(2)], got_mid[s])):
            z[s, k, HALO : tile - HALO, :] = value
        msg_link[s][EDGE].arrive()
        base = [jnp.where(turned(line, top), ns_in[s, p], ends(obj[s, p])) for p in range(2)]
        for k, value in enumerate(columns(base, got_edge[s])):
            z[s, k, :HALO, :] = value[:HALO]
            z[s, k, tile - HALO :, :] = value[HALO:]

    def back(s, gre, gim):
        east = jnp.where(lane64 < left - HALO, pack((gre, gim), 0), 0.0)
        west = jnp.where(lane64 >= left, pack((gre, gim), 1), 0.0)
        value = jnp.where(left > HALO, east, west)
        gmsg_edge[s] = ends(value)
        gmsg_link[s][EDGE].start()
        gmsg_mid[s] = value[HALO : tile - HALO]
        gmsg_link[s][MID].start()
        away = turned(line, top)
        lanes = lax.broadcasted_iota(jnp.int32, (1, tile), 1)
        stay = jnp.logical_not((lanes < left - HALO) | (lanes >= left + tile - HALO))
        for k, grad in enumerate((gre, gim)):
            grad = jnp.where(stay, grad, 0.0)
            acc_mid[s, k] = grad[HALO : tile - HALO]
            edge = ends(grad)
            acc_edge[s, k] = jnp.where(away, 0.0, edge)
            ns_out[s, k] = jnp.where(away, edge, 0.0)

    fetches[5].wait()
    assemble(0)
    ar, ai = z[0, 0], z[0, 1]
    pr, pi = probe[0], probe[1]
    vr, vi = sandwich(pr * ar - pi * ai, pr * ai + pi * ar, table, 1, False)

    for copy in rs_rows:
        copy.wait_recv()
    total = prev[row]
    for t in range(1, rows):
        total = total + buf1[t - 1]
    sum1[...] = total
    rs_cols = col_copies(0)
    for copy in rs_cols:
        copy.start()

    assemble(1)
    br, bi = z[1, 0], z[1, 1]
    wr, wi = sandwich(vr * br - vi * bi, vr * bi + vi * br, table, 0, False)
    fetches[6].wait()
    live = jnp.where(count[0] > 0, 2.0, 0.0)
    scale = live * (1.0 - amp[...] / jnp.sqrt(wr * wr + wi * wi + 1.0))
    xr, xi = sandwich(scale * wr, scale * wi, table, 0, True)
    back(1, xr * vr + xi * vi, xi * vr - xr * vi)

    for copy in rs_cols:
        copy.wait_recv()
    fetches[4].wait()
    total = sum1[col]
    for t in range(1, cols):
        total = total + buf2[t - 1]
    rate = PROBE_RATE / math.sqrt(rows * cols)
    newp[row, col] = probe_piece[...] - rate * total
    ag_cols = col_copies(1)
    for copy in ag_cols:
        copy.start()

    ur, ui = sandwich(xr * br + xi * bi, xi * br - xr * bi, table, 1, True)
    back(0, ur * pr + ui * pi, ui * pr - ur * pi)

    for s in (1,):
        for piece in (EDGE, MID):
            gmsg_link[s][piece].arrive()
            pass_link[s][piece].start()

    for copy in ag_cols:
        copy.wait_recv()
    ag_rows = row_copies(1)
    for copy in ag_rows:
        copy.start()

    for s in (0,):
        for piece in (EDGE, MID):
            gmsg_link[s][piece].arrive()
            pass_link[s][piece].start()

    home_rows = lax.rem(tile + HALO - top, tile)
    home_cols = lax.rem(tile + HALO - left, tile)
    part[0] = pltpu.roll(pltpu.roll(ur * ar + ui * ai, home_rows, 0), home_cols, 1)
    part[1] = pltpu.roll(pltpu.roll(ui * ar - ur * ai, home_rows, 0), home_cols, 1)
    part_out = pltpu.make_async_copy(part, out_part, out_sem.at[0])
    part_out.start()

    head_off, tail_off = off[0], off[1]
    accept = (head_off[1, :1] > HALO, tail_off[1, :1] < HALO)
    corner = (head_off[0, :1], tail_off[0, :1])
    span = (slice(0, wide), slice(tile - wide, tile))

    def parts_of(slot, strip):
        if slot == 0:
            return jnp.where(first, strip, 0.0), jnp.where(first, swap(strip), 0.0)
        return jnp.where(first, 0.0, swap(strip)), jnp.where(first, 0.0, strip)

    def collect_edge(s):
        pass_link[s][EDGE].arrive()
        for slot in range(2):
            strip = jnp.where(accept[slot], gs_edge[slot, s], 0.0)
            moves = turned(line, corner[slot])
            for dst, kept in ((ns_out, jnp.where(moves, strip, 0.0)), (acc_edge, jnp.where(moves, 0.0, strip))):
                for k, value in enumerate(parts_of(slot, kept)):
                    dst[s, k, :, span[slot]] += value
        for link in ns[1][s]:
            link.start()

    writes = []

    def collect_mid(s):
        pass_link[s][MID].arrive()
        for slot in range(2):
            strip = jnp.where(accept[slot], gs_mid[slot, s], 0.0)
            for k, value in enumerate(parts_of(slot, strip)):
                acc_mid[s, k, :, span[slot]] += value
        for k in range(2):
            new_mid[s, k] = obj[s, k, HALO : tile - HALO, :] - OBJ_RATE * acc_mid[s, k]
        copy = pltpu.make_async_copy(new_mid.at[s], out_obj.at[s, :, HALO : tile - HALO, :], out_sem.at[1 + s])
        copy.start()
        writes.append(copy)

    def finish_edge(s):
        for link in ns[1][s]:
            link.arrive()
        for k in range(2):
            new_edge[s, k] = ends(obj[s, k]) - OBJ_RATE * (acc_edge[s, k] + ns_back[s, k])
        for k, (src, dst) in enumerate(((up, up), (down, slice(tile - HALO, tile)))):
            copy = pltpu.make_async_copy(new_edge.at[s, :, src, :], out_obj.at[s, :, dst, :], out_sem.at[3 + 2 * s + k])
            copy.start()
            writes.append(copy)

    collect_edge(1)
    collect_edge(0)
    collect_mid(1)
    collect_mid(0)
    finish_edge(1)
    for copy in ag_rows:
        copy.wait_recv()
    probe_out = pltpu.make_async_copy(newp, out_probe, out_sem.at[7])
    probe_out.start()
    finish_edge(0)

    off_near.sent()
    off_far.sent()
    for s in range(2):
        for phase in range(2):
            for link in ns[phase][s]:
                link.sent()
        for piece in range(2):
            for group in (far_link, msg_link, gmsg_link, pass_link):
                group[s][piece].sent()
    for copy in rs_rows + rs_cols + ag_cols + ag_rows:
        copy.wait_send()
    part_out.wait()
    for copy in writes:
        copy.wait()
    probe_out.wait()


def shards(rows, cols, objects, probe, prev_partial, offsets, counts, amplitudes):
    tile = objects.shape[2]
    win = probe.shape[-1]
    assert tile == win and cols % 2 == 0
    piece = (2 * win) // (rows * cols)
    split_shape = (rows, cols, piece, win)
    table = jnp.asarray(operator_table(win))
    f32 = jnp.float32
    smem = pl.BlockSpec(memory_space=pltpu.SMEM)
    anyspace = pl.BlockSpec(memory_space=pl.ANY)
    V = lambda *shape: pltpu.VMEM(shape, f32)
    mid, wide = tile - 2 * HALO, 2 * HALO
    dma = pltpu.SemaphoreType.DMA
    scratch = [
        V(2, 2, tile, tile), V(*split_shape), V(2, win, win), V(piece, win), V(win, win),
        pltpu.VMEM(table.shape, jnp.bfloat16),
        pltpu.VMEM((2, 8, wide), jnp.int32), pltpu.VMEM((2, 2, 8, wide), jnp.int32),
        V(2, 2, wide, tile), V(2, 2, mid, wide), V(2, 2, wide, wide), V(2, wide, wide),
        V(2, mid, wide), V(2, wide, wide), V(2, mid, wide), V(2, wide, wide), V(2, mid, wide), V(2, wide, wide),
        V(2, 2, tile, tile),
        V(2, mid, wide), V(2, wide, wide), V(2, 2, mid, wide), V(2, 2, wide, wide),
        V(2, 2, mid, tile), V(2, 2, wide, tile), V(2, 2, wide, tile), V(2, 2, wide, tile),
        V(2, 2, mid, tile), V(2, 2, wide, tile), V(2, win, win),
        V(max(rows - 1, 1), cols, piece, win), V(cols, piece, win),
        V(max(cols - 1, 1), piece, win), V(*split_shape),
        dma((7,)), dma((8,)), dma((2,)), dma((2,)), dma((2, 2, 2)), dma((2, 2, 2)),
        dma((2, 2, 2)), dma((2, 2, 2)), dma((2, 2, 2)), dma((2, 2, 2)),
        dma((2, max(rows - 1, 1))), dma((2, max(rows - 1, 1))),
        dma((2, max(cols - 1, 1))), dma((2, max(cols - 1, 1))),
        pltpu.SemaphoreType.REGULAR((max(cols.bit_length() - 2, 1),)),
    ]
    new_obj, new_probe, part = pl.pallas_call(
        functools.partial(kernel, rows, cols),
        out_shape=(
            jax.ShapeDtypeStruct(objects.shape, f32),
            jax.ShapeDtypeStruct(split_shape, f32),
            jax.ShapeDtypeStruct(probe.shape, f32),
        ),
        in_specs=[smem, smem] + [anyspace] * 6,
        out_specs=(anyspace, anyspace, anyspace),
        scratch_shapes=scratch,
        compiler_params=pltpu.CompilerParams(
            collective_id=0, has_side_effects=True, vmem_limit_bytes=56 * 2**20
        ),
    )(
        offsets.reshape(2), counts.reshape(1), objects, prev_partial.reshape(split_shape),
        probe, probe.reshape(split_shape), amplitudes.reshape(win, win), table,
    )
    return new_obj, new_probe.reshape(probe.shape), part[None, None]


def solution(mesh):
    in_specs = (
        P(None, None, "row", "col"),
        P(),
        P("row", "col", None, None, None),
        P("row", "col", None, None),
        P("row", "col"),
        P("row", "col", None, None, None),
    )
    out_specs = (P(None, None, "row", "col"), P(), P("row", "col", None, None, None))
    body = functools.partial(shards, mesh.shape["row"], mesh.shape["col"])
    return jax.shard_map(body, mesh=mesh, in_specs=in_specs, out_specs=out_specs, check_vma=False)
```

profile of v0, /device:TPU:1, one launch (start us, length us, event | category | flops | bytes accessed | tf_op | source)
XLA Modules:
  0.0 42.4 jit_solution(3476891822417169758)
XLA Ops:
  1.3 37.1 %shard_map.94 = (f32[2,2,256,256]{3,2,1,0:T(8,128)}, f32[4,8,16,256]{3,2,1,0:T(8,128)}, f32[2,256,256]{2,1,0:T(8,128)}) custom-call(s32[2]{0:T(128)} %bitcast.13, s32[1]{0:T(128)} %bitcast.7.count, f32[2,2,256,256]{3,2,1,0:T(8,128)} %obj_hbm.1, f32[4,8,16,256]{3,2,1,0:T(8,128)} %bitcast.9, f32[2,256,256]{2,1,0:T(8,128)} %probe_hbm.1, ...), custom_call_target="tpu_custom_call" | custom-call | tf_op jit(solution)/shard_map/pallas_call | solution.py:542
  38.4 0.0 copy-start.1
  38.4 0.0 copy-start
  38.4 2.4 %copy.14 = f32[2,2,256,256]{3,2,1,0:T(8,128)} copy(f32[2,2,256,256]{3,2,1,0:T(8,128)} %get-tuple-element.12) | data formatting | bytes 2097152
  40.8 0.0 copy-done.1
  40.8 0.8 %copy.15 = f32[2,256,256]{2,1,0:T(8,128)} copy(f32[2,256,256]{2,1,0:T(8,128)S(1)} %bitcast.11) | data formatting | bytes 1048576
  41.6 0.0 copy-done
  41.6 0.8 %copy.16 = f32[1,1,2,256,256]{4,3,2,1,0:T(8,128)} copy(f32[1,1,2,256,256]{4,3,2,1,0:T(8,128)S(1)} %bitcast.10) | data formatting | bytes 1048576
Async XLA Ops:
  38.4 2.4 %copy-start.1 = (f32[4,8,16,256]{3,2,1,0:T(8,128)S(1)}, f32[4,8,16,256]{3,2,1,0:T(8,128)}, u32[]{:S(2)}) copy-start(f32[4,8,16,256]{3,2,1,0:T(8,128)} %get-tuple-element.7) | copy-start | bytes 1572868
  38.4 3.2 %copy-start = (f32[2,256,256]{2,1,0:T(8,128)S(1)}, f32[2,256,256]{2,1,0:T(8,128)}, u32[]{:S(2)}) copy-start(f32[2,256,256]{2,1,0:T(8,128)} %get-tuple-element.8) | copy-start | bytes 1572868
where the time goes:
time: 42.9 us; the launch traced here: 42.4 us
  Pallas kernels  37.1 us (86%)
  local copies, waits for them, and re-layouts  3.97 us (9%)
  between operations  1.3 us (3%)
    pallas_call x1, Pallas kernels, shards(): pl.pallas_call(functools.partial(kernel, rows, cols), out_shape=(jax.Shap...  37.1 us
    unnamed x7, local copies, waits for them, and re-layouts  3.97 us

commit v1 on v0

--- a/solution.py
+++ b/solution.py
@@ -22,20 +22,20 @@
 
 
 def operator_table(n):
+    half = n // 2
     index = np.arange(n)
-    angle = 2.0 * np.pi * (np.outer(index, index) % n) / n
-    dft = np.exp(-1j * angle) / np.sqrt(n)
-    freq = np.where(index < n // 2, index, index - n).astype(np.float64)
+    dft = np.exp(-2j * np.pi * (np.outer(index, index) % n) / n) / np.sqrt(n)
+    freq = np.where(index < half, index, index - n).astype(np.float64)
     phase = np.exp(1j * np.pi * freq * freq / (4.0 * n))
     prop = np.conj(dft) @ (phase[:, None] * dft)
+    near, far = prop[:half, :half], prop[:half, half:]
     tables = []
-    for mat in (dft, prop):
-        for part in (mat.real, mat.imag, -mat.imag):
-            part = part.astype(np.float32)
+    for mat in (dft[0::2, :half], dft[1::2, :half], (near + far) / 2, (near - far) / 2):
+        right = np.block([[mat.real.T, mat.imag.T], [-mat.imag.T, mat.real.T]]).astype(np.float32)
+        for part in (right, right.T):
             high = part.astype(jnp.bfloat16)
-            low = (part - high.astype(np.float32)).astype(jnp.bfloat16)
-            tables += [high, low]
-    return np.stack(tables).reshape(2, 3, 2, n, n)
+            tables += [high, (part - high.astype(np.float32)).astype(jnp.bfloat16)]
+    return np.stack(tables).reshape(2, 2, 2, 2, n, n)
 
 
 def dot(left, right):
@@ -46,22 +46,42 @@
     return jnp.concatenate(parts, axis=axis)
 
 
+def times(data, table, which, side, flip):
+    kind = int(flip if side else not flip)
+    out = []
+    for k in range(2):
+        high, low = table[which, k, kind, 0], table[which, k, kind, 1]
+        dh, dl = split(data[k])
+        if side:
+            out.append(dot(cat([dh, dl, dh], 1), cat([high, high, low], 0)))
+        else:
+            out.append(dot(cat([high, high, low], 1), cat([dh, dl, dh], 0)))
+    return out
+
+
+def halves(value, axis):
+    half = value.shape[axis] // 2
+    return (value[:half], value[half:]) if axis == 0 else (value[:, :half], value[:, half:])
+
+
+def transform(re, im, table, which, axis, merge, divide, flip):
+    if divide:
+        parts = [halves(v, axis) for v in (re, im)]
+        data = [cat([a + b for a, b in parts], axis), cat([a - b for a, b in parts], axis)]
+    else:
+        parts = [halves(v, axis) for v in (re, im)]
+        data = [cat([p[0] for p in parts], axis), cat([p[1] for p in parts], axis)]
+    even, odd = [halves(v, axis) for v in times(data, table, which, axis, flip)]
+    if merge:
+        return [cat([a + b, a - b], axis) for a, b in zip(even, odd)]
+    return [cat([a, b], axis) for a, b in zip(even, odd)]
+
+
 def sandwich(xr, xi, table, which, conj):
-    re, im, neg = table.at[which, 0], table.at[which, 1], table.at[which, 2]
-    if conj:
-        im, neg = neg, im
-    rh, rl, ih, il, nh, nl = (p[k] for p in (re, im, neg) for k in (0, 1))
-    xrh, xrl = split(xr)
-    xih, xil = split(xi)
-    left = cat([xrh, xih, xrl, xil, xrh, xih], 1)
-    tr = dot(left, cat([rh, nh, rh, nh, rl, nl], 0))
-    ti = dot(left, cat([ih, rh, ih, rh, il, rl], 0))
-    trh, trl = split(tr)
-    tih, til = split(ti)
-    right = cat([trh, tih, trl, til, trh, tih], 0)
-    yr = dot(cat([rh, nh, rh, nh, rl, nl], 1), right)
-    yi = dot(cat([ih, rh, ih, rh, il, rl], 1), right)
-    return yr, yi
+    divide = which == 1 or not conj
+    merge = which == 1 or conj
+    tr, ti = transform(xr, xi, table, which, 1, merge, divide, conj)
+    return transform(tr, ti, table, which, 0, merge, divide, conj)
 
 
 def kernel(
@@ -70,9 +90,9 @@
     obj, prev, probe, probe_piece, amp, table,
     my_off, off,
     ns_in, strip_mid, strip_edge, fold_far, far_mid, far_edge, msg_mid, msg_edge, got_mid, got_edge, z,
-    gmsg_mid, gmsg_edge, gs_mid, gs_edge, acc_mid, acc_edge, ns_out, ns_back, new_mid, new_edge, part,
-    buf1, sum1, buf2, newp,
-    local_sem, out_sem, off_send, off_recv, ns_send, ns_recv, far_send, far_recv, msg_send, msg_recv,
+    gmsg_mid, gmsg_edge, gs_mid, gs_edge, acc_mid, acc_edge, ns_out, ns_back,
+    buf1, buf2,
+    local_sem, off_send, off_recv, ns_send, ns_recv, far_send, far_recv, msg_send, msg_recv,
     row_send, row_recv, col_send, col_recv, known,
 ):
     tile = obj.shape[2]
@@ -91,11 +111,36 @@
     has_north, has_south = row > 0, row < rows - 1
     always = row >= 0
 
+    def flip(value, bit):
+        return value + bit * (1 - 2 * lax.rem(value // bit, 2))
+
+    row_bits = [1 << k for k in range(rows.bit_length() - 1)]
+    base, length, row_down, row_keep = 0, rows, [], []
+    for k, bit in enumerate(row_bits):
+        length = length // 2
+        upper = lax.rem(row // bit, 2)
+        keep, give = base + upper * length, base + (1 - upper) * length
+        landing = buf1.at[pl.ds(rows - 2 * length, length)]
+        row_down.append(pltpu.make_async_remote_copy(
+            src_ref=prev.at[pl.ds(give, length)], dst_ref=landing, send_sem=row_send.at[0, k],
+            recv_sem=row_recv.at[0, k], device_id=(flip(row, bit), col), device_id_type=MESH))
+        row_keep.append((keep, length, landing))
+        base = keep
+    slot = base
+    row_up = []
+    for k, bit in enumerate(reversed(row_bits)):
+        here = out_probe.at[pl.ds(base, length)]
+        row_up.append(pltpu.make_async_remote_copy(
+            src_ref=here, dst_ref=here, send_sem=row_send.at[1, k],
+            recv_sem=row_recv.at[1, k], device_id=(flip(row, bit), col), device_id_type=MESH))
+        base = base - length * lax.rem(row // bit, 2)
+        length = 2 * length
+
     fetches = [
         pltpu.make_async_copy(src, dst, local_sem.at[k])
         for k, (src, dst) in enumerate(
             ((obj_hbm.at[0], obj.at[0]), (obj_hbm.at[1], obj.at[1]), (prev_hbm, prev),
-             (probe_hbm, probe), (probe_k_hbm.at[row, col], probe_piece),
+             (probe_hbm, probe), (probe_k_hbm.at[slot, col], probe_piece),
              (table_hbm, table), (amp_hbm, amp))
         )
     ]
@@ -106,9 +151,6 @@
 
     def greet(sem, r, c):
         pl.semaphore_signal(sem, inc=1, device_id=(r, c), device_id_type=MESH)
-
-    def flip(value, bit):
-        return value + bit * (1 - 2 * lax.rem(value // bit, 2))
 
     bits = [1 << k for k in range(cols.bit_length() - 1)]
     expected = 0
@@ -150,15 +192,27 @@
 
     for s in range(2):
         fetches[s].wait()
-        for slot in range(2):
-            value = pack((obj[s, 0], obj[s, 1]), slot)
-            strip_mid[slot, s] = value[HALO : tile - HALO]
-            strip_edge[slot, s] = ends(value)
+        for side in range(2):
+            value = pack((obj[s, 0], obj[s, 1]), side)
+            strip_mid[side, s] = value[HALO : tile - HALO]
+            strip_edge[side, s] = ends(value)
     fetches[3].wait()
     turn_rows = lax.rem(top + tile - HALO, tile)
     turn_cols = lax.rem(left + tile - HALO, tile)
     for k in range(2):
         probe[k] = pltpu.roll(pltpu.roll(probe[k], turn_rows, 0), turn_cols, 1)
+
+    fetches[6].wait()
+    count_half = tile // 2
+
+    def order(axis):
+        target = lax.broadcasted_iota(jnp.int32, (tile, tile), axis)
+        source = lax.broadcasted_iota(jnp.int32, (tile, tile), 1 - axis)
+        target = jnp.where(target < count_half, 2 * target, 2 * (target - count_half) + 1)
+        return (source == target).astype(jnp.float32).astype(jnp.bfloat16)
+
+    ordered = dot(cat([order(0), order(0)], 1), cat(split(amp[...]), 0))
+    amp[...] = dot(cat(split(ordered), 1), cat([order(1), order(1)], 0))
 
     @pl.when(jnp.logical_not(has_other))
     def _():
@@ -254,27 +308,19 @@
         for s in range(2)
     ]
 
-    def row_copies(stage):
-        made = []
-        for t in range(1, rows):
-            peer = lax.rem(row + t, rows)
-            if stage == 0:
-                src, dst = prev.at[peer], buf1.at[t - 1]
-            else:
-                src, dst = newp.at[row], newp.at[row]
-            made.append(pltpu.make_async_remote_copy(
-                src_ref=src, dst_ref=dst, send_sem=row_send.at[stage, t - 1],
-                recv_sem=row_recv.at[stage, t - 1], device_id=(peer, col), device_id_type=MESH))
-        return made
+    def add_rows(k):
+        keep, count_rows, landing = row_keep[k]
+        row_down[k].wait_recv()
+        prev[pl.ds(keep, count_rows)] += landing[...]
 
     def col_copies(stage):
         made = []
         for t in range(1, cols):
             peer = lax.rem(col + t, cols)
             if stage == 0:
-                src, dst = sum1.at[peer], buf2.at[t - 1]
+                src, dst = prev.at[slot, peer], buf2.at[t - 1]
             else:
-                src, dst = newp.at[row, col], newp.at[row, col]
+                src, dst = out_probe.at[slot, col], out_probe.at[slot, col]
             made.append(pltpu.make_async_remote_copy(
                 src_ref=src, dst_ref=dst, send_sem=col_send.at[stage, t - 1],
                 recv_sem=col_recv.at[stage, t - 1], device_id=(row, peer), device_id_type=MESH))
@@ -285,13 +331,11 @@
 
     off_near.start()
     off_far.start()
+    row_down[0].start()
     for s in range(2):
         for link in ns[0][s]:
             link.start()
         far_link[s][MID].start()
-    rs_rows = row_copies(0)
-    for copy in rs_rows:
-        copy.start()
     for bit in bits:
         greet(known.at[0], row, flip(col, bit))
 
@@ -322,11 +366,17 @@
         msg_edge[s] = jnp.where(take_own, msg_edge[s], far_edge[s])
         msg_link[s][EDGE].start()
 
-    for s in range(2):
-        fold(s)
-        forward_mid(s)
-    for s in range(2):
-        forward_edge(s)
+    fold(0)
+    forward_mid(0)
+    add_rows(0)
+    for k in range(1, len(row_bits)):
+        row_down[k].start()
+        if k + 1 < len(row_bits):
+            add_rows(k)
+    fold(1)
+    forward_mid(1)
+    forward_edge(0)
+    forward_edge(1)
 
     for wait_round, bit in enumerate(bits[1:]):
         pl.semaphore_wait(known.at[wait_round], len(bits))
@@ -372,42 +422,37 @@
             acc_edge[s, k] = jnp.where(away, 0.0, edge)
             ns_out[s, k] = jnp.where(away, edge, 0.0)
 
+    if len(row_bits) > 1:
+        add_rows(len(row_bits) - 1)
+    rs_cols = col_copies(0)
+    for copy in rs_cols:
+        copy.start()
+
     fetches[5].wait()
     assemble(0)
     ar, ai = z[0, 0], z[0, 1]
     pr, pi = probe[0], probe[1]
     vr, vi = sandwich(pr * ar - pi * ai, pr * ai + pi * ar, table, 1, False)
 
-    for copy in rs_rows:
-        copy.wait_recv()
-    total = prev[row]
-    for t in range(1, rows):
-        total = total + buf1[t - 1]
-    sum1[...] = total
-    rs_cols = col_copies(0)
-    for copy in rs_cols:
-        copy.start()
-
     assemble(1)
     br, bi = z[1, 0], z[1, 1]
     wr, wi = sandwich(vr * br - vi * bi, vr * bi + vi * br, table, 0, False)
-    fetches[6].wait()
-    live = jnp.where(count[0] > 0, 2.0, 0.0)
-    scale = live * (1.0 - amp[...] / jnp.sqrt(wr * wr + wi * wi + 1.0))
-    xr, xi = sandwich(scale * wr, scale * wi, table, 0, True)
-    back(1, xr * vr + xi * vi, xi * vr - xr * vi)
-
     for copy in rs_cols:
         copy.wait_recv()
     fetches[4].wait()
-    total = sum1[col]
+    total = prev[slot, col]
     for t in range(1, cols):
         total = total + buf2[t - 1]
     rate = PROBE_RATE / math.sqrt(rows * cols)
-    newp[row, col] = probe_piece[...] - rate * total
+    out_probe[slot, col] = probe_piece[...] - rate * total
     ag_cols = col_copies(1)
     for copy in ag_cols:
         copy.start()
+
+    live = jnp.where(count[0] > 0, 2.0, 0.0)
+    scale = live - (live * amp[...]) * lax.rsqrt(wr * wr + wi * wi + 1.0)
+    xr, xi = sandwich(scale * wr, scale * wi, table, 0, True)
+    back(1, xr * vr + xi * vi, xi * vr - xr * vi)
 
     ur, ui = sandwich(xr * br + xi * bi, xi * br - xr * bi, table, 1, True)
     back(0, ur * pr + ui * pi, ui * pr - ur * pi)
@@ -419,9 +464,7 @@
 
     for copy in ag_cols:
         copy.wait_recv()
-    ag_rows = row_copies(1)
-    for copy in ag_rows:
-        copy.start()
+    row_up[0].start()
 
     for s in (0,):
         for piece in (EDGE, MID):
@@ -430,10 +473,8 @@
 
     home_rows = lax.rem(tile + HALO - top, tile)
     home_cols = lax.rem(tile + HALO - left, tile)
-    part[0] = pltpu.roll(pltpu.roll(ur * ar + ui * ai, home_rows, 0), home_cols, 1)
-    part[1] = pltpu.roll(pltpu.roll(ui * ar - ur * ai, home_rows, 0), home_cols, 1)
-    part_out = pltpu.make_async_copy(part, out_part, out_sem.at[0])
-    part_out.start()
+    out_part[0] = pltpu.roll(pltpu.roll(ur * ar + ui * ai, home_rows, 0), home_cols, 1)
+    out_part[1] = pltpu.roll(pltpu.roll(ui * ar - ur * ai, home_rows, 0), home_cols, 1)
 
     head_off, tail_off = off[0], off[1]
     accept = (head_off[1, :1] > HALO, tail_off[1, :1] < HALO)
@@ -456,8 +497,6 @@
         for link in ns[1][s]:
             link.start()
 
-    writes = []
-
     def collect_mid(s):
         pass_link[s][MID].arrive()
         for slot in range(2):
@@ -465,30 +504,25 @@
             for k, value in enumerate(parts_of(slot, strip)):
                 acc_mid[s, k, :, span[slot]] += value
         for k in range(2):
-            new_mid[s, k] = obj[s, k, HALO : tile - HALO, :] - OBJ_RATE * acc_mid[s, k]
-        copy = pltpu.make_async_copy(new_mid.at[s], out_obj.at[s, :, HALO : tile - HALO, :], out_sem.at[1 + s])
-        copy.start()
-        writes.append(copy)
+            out_obj[s, k, HALO : tile - HALO, :] = obj[s, k, HALO : tile - HALO, :] - OBJ_RATE * acc_mid[s, k]
 
     def finish_edge(s):
         for link in ns[1][s]:
             link.arrive()
         for k in range(2):
-            new_edge[s, k] = ends(obj[s, k]) - OBJ_RATE * (acc_edge[s, k] + ns_back[s, k])
-        for k, (src, dst) in enumerate(((up, up), (down, slice(tile - HALO, tile)))):
-            copy = pltpu.make_async_copy(new_edge.at[s, :, src, :], out_obj.at[s, :, dst, :], out_sem.at[3 + 2 * s + k])
-            copy.start()
-            writes.append(copy)
+            value = ends(obj[s, k]) - OBJ_RATE * (acc_edge[s, k] + ns_back[s, k])
+            out_obj[s, k, :HALO, :] = value[:HALO]
+            out_obj[s, k, tile - HALO :, :] = value[HALO:]
 
     collect_edge(1)
     collect_edge(0)
     collect_mid(1)
     collect_mid(0)
+    for k in range(1, len(row_bits)):
+        row_up[k - 1].wait_recv()
+        row_up[k].start()
     finish_edge(1)
-    for copy in ag_rows:
-        copy.wait_recv()
-    probe_out = pltpu.make_async_copy(newp, out_probe, out_sem.at[7])
-    probe_out.start()
+    row_up[-1].wait_recv()
     finish_edge(0)
 
     off_near.sent()
@@ -500,12 +534,19 @@
         for piece in range(2):
             for group in (far_link, msg_link, gmsg_link, pass_link):
                 group[s][piece].sent()
-    for copy in rs_rows + rs_cols + ag_cols + ag_rows:
+    for copy in row_down + rs_cols + ag_cols + row_up:
         copy.wait_send()
-    part_out.wait()
-    for copy in writes:
+
+
+def store(obj, probe, part, out_obj, out_probe, out_part, sem):
+    copies = [
+        pltpu.make_async_copy(src, dst, sem.at[k])
+        for k, (src, dst) in enumerate(((obj, out_obj), (probe, out_probe), (part, out_part)))
+    ]
+    for copy in copies:
+        copy.start()
+    for copy in copies:
         copy.wait()
-    probe_out.wait()
 
 
 def shards(rows, cols, objects, probe, prev_partial, offsets, counts, amplitudes):
@@ -518,6 +559,7 @@
     f32 = jnp.float32
     smem = pl.BlockSpec(memory_space=pltpu.SMEM)
     anyspace = pl.BlockSpec(memory_space=pl.ANY)
+    vmem = pl.BlockSpec(memory_space=pltpu.VMEM)
     V = lambda *shape: pltpu.VMEM(shape, f32)
     mid, wide = tile - 2 * HALO, 2 * HALO
     dma = pltpu.SemaphoreType.DMA
@@ -530,24 +572,20 @@
         V(2, 2, tile, tile),
         V(2, mid, wide), V(2, wide, wide), V(2, 2, mid, wide), V(2, 2, wide, wide),
         V(2, 2, mid, tile), V(2, 2, wide, tile), V(2, 2, wide, tile), V(2, 2, wide, tile),
-        V(2, 2, mid, tile), V(2, 2, wide, tile), V(2, win, win),
-        V(max(rows - 1, 1), cols, piece, win), V(cols, piece, win),
-        V(max(cols - 1, 1), piece, win), V(*split_shape),
-        dma((7,)), dma((8,)), dma((2,)), dma((2,)), dma((2, 2, 2)), dma((2, 2, 2)),
+        V(max(rows - 1, 1), cols, piece, win), V(max(cols - 1, 1), piece, win),
+        dma((7,)), dma((2,)), dma((2,)), dma((2, 2, 2)), dma((2, 2, 2)),
         dma((2, 2, 2)), dma((2, 2, 2)), dma((2, 2, 2)), dma((2, 2, 2)),
         dma((2, max(rows - 1, 1))), dma((2, max(rows - 1, 1))),
         dma((2, max(cols - 1, 1))), dma((2, max(cols - 1, 1))),
         pltpu.SemaphoreType.REGULAR((max(cols.bit_length() - 2, 1),)),
     ]
-    new_obj, new_probe, part = pl.pallas_call(
+    results = pl.pallas_call(
         functools.partial(kernel, rows, cols),
         out_shape=(
-            jax.ShapeDtypeStruct(objects.shape, f32),
-            jax.ShapeDtypeStruct(split_shape, f32),
-            jax.ShapeDtypeStruct(probe.shape, f32),
+            pltpu.VMEM(objects.shape, f32), pltpu.VMEM(split_shape, f32), pltpu.VMEM(probe.shape, f32),
         ),
         in_specs=[smem, smem] + [anyspace] * 6,
-        out_specs=(anyspace, anyspace, anyspace),
+        out_specs=(vmem, vmem, vmem),
         scratch_shapes=scratch,
         compiler_params=pltpu.CompilerParams(
             collective_id=0, has_side_effects=True, vmem_limit_bytes=56 * 2**20
@@ -556,6 +594,13 @@
         offsets.reshape(2), counts.reshape(1), objects, prev_partial.reshape(split_shape),
         probe, probe.reshape(split_shape), amplitudes.reshape(win, win), table,
     )
+    new_obj, new_probe, part = pl.pallas_call(
+        store,
+        out_shape=tuple(jax.ShapeDtypeStruct(v.shape, f32) for v in results),
+        in_specs=[vmem] * 3,
+        out_specs=(pl.BlockSpec(memory_space=pltpu.HBM),) * 3,
+        scratch_shapes=[dma((3,))],
+    )(*[pltpu.with_memory_space_constraint(v, pltpu.VMEM) for v in results])
     return new_obj, new_probe.reshape(probe.shape), part[None, None]
 
 

time: 42.9 us -> 37.9 us (0.88)
  local copies, waits for them, and re-layouts: 3.97 us -> 0 us
  Pallas kernels: 37.1 us -> 36.4 us
    unnamed x7 -> x0, local copies, waits for them, and re-layouts: 3.97 us -> none
    pallas_call x1 -> x2, Pallas kernels: 37.1 us -> 36.4 us  [the longest x1 35.1 us: shards(): pl.pallas_call(functools.partial(kernel, rows, cols), out_shape=(pltpu.VM...]
where the time goes in v1:
time: 37.9 us; the launch traced here: 37.7 us
  Pallas kernels  36.4 us (96%)
  between operations  1.29 us (3%)
    pallas_call x1, Pallas kernels, shards(): pl.pallas_call(functools.partial(kernel, rows, cols), out_shape=(pltpu.VM...  35.1 us
    pallas_call x1, Pallas kernels, shards(): pl.pallas_call(store, out_shape=tuple((jax.ShapeDtypeStruct(v.shape, f32)...  1.34 us

profile of v1, /device:TPU:1, one launch (start us, length us, event | category | flops | bytes accessed | tf_op | source)
XLA Modules:
  0.0 37.7 jit_solution(11905188183096359165)
XLA Ops:
  1.3 35.1 %shard_map.94 = (f32[2,2,256,256]{3,2,1,0:T(8,128)S(1)}, f32[4,8,16,256]{3,2,1,0:T(8,128)S(1)}, f32[2,256,256]{2,1,0:T(8,128)S(1)}) custom-call(s32[2]{0:T(128)} %bitcast.11, s32[1]{0:T(128)} %bitcast.7.count, f32[2,2,256,256]{3,2,1,0:T(8,128)} %obj_hbm.1, f32[4,8,16,256]{3,2,1,0:T(8,128)} %bitcast.9, f32[2,256,256]{2,1,0:T(8,128)} %probe_hbm.1, ...), custom_call_target="tpu_custom_call" | custom-call | tf_op jit(solution)/shard_map/pallas_call | solution.py:582
  36.4 1.3 %shard_map.95 = (f32[2,2,256,256]{3,2,1,0:T(8,128)}, f32[4,8,16,256]{3,2,1,0:T(8,128)}, f32[2,256,256]{2,1,0:T(8,128)}) custom-call(f32[2,2,256,256]{3,2,1,0:T(8,128)S(1)} %get-tuple-element.9.obj, f32[4,8,16,256]{3,2,1,0:T(8,128)S(1)} %get-tuple-element.10.probe, f32[2,256,256]{2,1,0:T(8,128)S(1)} %get-tuple-element.11.part), custom_call_target="tpu_custom_call" | custom-call | tf_op jit(solution)/shard_map/pallas_call | solution.py:597

commit v2 on v1

--- a/solution.py
+++ b/solution.py
@@ -127,14 +127,22 @@
         row_keep.append((keep, length, landing))
         base = keep
     slot = base
-    row_up = []
+    row_up = {}
     for k, bit in enumerate(reversed(row_bits)):
-        here = out_probe.at[pl.ds(base, length)]
-        row_up.append(pltpu.make_async_remote_copy(
-            src_ref=here, dst_ref=here, send_sem=row_send.at[1, k],
-            recv_sem=row_recv.at[1, k], device_id=(flip(row, bit), col), device_id_type=MESH))
-        base = base - length * lax.rem(row // bit, 2)
-        length = 2 * length
+        for held in range(1 << k):
+            where = slot
+            for t in range(k):
+                where = flip(where, 1 << t) if held >> t & 1 else where
+            here, index = out_probe.at[where], held | 1 << k
+            row_up[index] = pltpu.make_async_remote_copy(
+                src_ref=here, dst_ref=here, send_sem=row_send.at[1, index - 1],
+                recv_sem=row_recv.at[1, index - 1], device_id=(flip(row, bit), col), device_id_type=MESH)
+
+    def spread_rows(held):
+        if held:
+            row_up[held].wait_recv()
+        for k in range(held.bit_length(), len(row_bits)):
+            row_up[held | 1 << k].start()
 
     fetches = [
         pltpu.make_async_copy(src, dst, local_sem.at[k])
@@ -366,13 +374,13 @@
         msg_edge[s] = jnp.where(take_own, msg_edge[s], far_edge[s])
         msg_link[s][EDGE].start()
 
-    fold(0)
-    forward_mid(0)
     add_rows(0)
     for k in range(1, len(row_bits)):
         row_down[k].start()
         if k + 1 < len(row_bits):
             add_rows(k)
+    fold(0)
+    forward_mid(0)
     fold(1)
     forward_mid(1)
     forward_edge(0)
@@ -437,6 +445,11 @@
     assemble(1)
     br, bi = z[1, 0], z[1, 1]
     wr, wi = sandwich(vr * br - vi * bi, vr * bi + vi * br, table, 0, False)
+    live = jnp.where(count[0] > 0, 2.0, 0.0)
+    scale = live - (live * amp[...]) * lax.rsqrt(wr * wr + wi * wi + 1.0)
+    xr, xi = sandwich(scale * wr, scale * wi, table, 0, True)
+    back(1, xr * vr + xi * vi, xi * vr - xr * vi)
+
     for copy in rs_cols:
         copy.wait_recv()
     fetches[4].wait()
@@ -449,10 +462,6 @@
     for copy in ag_cols:
         copy.start()
 
-    live = jnp.where(count[0] > 0, 2.0, 0.0)
-    scale = live - (live * amp[...]) * lax.rsqrt(wr * wr + wi * wi + 1.0)
-    xr, xi = sandwich(scale * wr, scale * wi, table, 0, True)
-    back(1, xr * vr + xi * vi, xi * vr - xr * vi)
 
     ur, ui = sandwich(xr * br + xi * bi, xi * br - xr * bi, table, 1, True)
     back(0, ur * pr + ui * pi, ui * pr - ur * pi)
@@ -464,7 +473,7 @@
 
     for copy in ag_cols:
         copy.wait_recv()
-    row_up[0].start()
+    spread_rows(0)
 
     for s in (0,):
         for piece in (EDGE, MID):
@@ -516,13 +525,11 @@
 
     collect_edge(1)
     collect_edge(0)
+    for held in range(1, rows):
+        spread_rows(held)
     collect_mid(1)
     collect_mid(0)
-    for k in range(1, len(row_bits)):
-        row_up[k - 1].wait_recv()
-        row_up[k].start()
     finish_edge(1)
-    row_up[-1].wait_recv()
     finish_edge(0)
 
     off_near.sent()
@@ -534,7 +541,7 @@
         for piece in range(2):
             for group in (far_link, msg_link, gmsg_link, pass_link):
                 group[s][piece].sent()
-    for copy in row_down + rs_cols + ag_cols + row_up:
+    for copy in row_down + rs_cols + ag_cols + list(row_up.values()):
         copy.wait_send()
 
 

time: 37.9 us -> 35.8 us (0.945)
  Pallas kernels: 36.4 us -> 34.1 us
    pallas_call x1, Pallas kernels: 35.1 us -> 32.8 us  [shards(): pl.pallas_call(functools.partial(kernel, rows, cols), out_shape=(pltpu.VM...]
where the time goes in v2:
time: 35.8 us; the launch traced here: 35.4 us
  Pallas kernels  34.1 us (95%)
  between operations  1.29 us (4%)
    pallas_call x1, Pallas kernels, shards(): pl.pallas_call(functools.partial(kernel, rows, cols), out_shape=(pltpu.VM...  32.8 us
    pallas_call x1, Pallas kernels, shards(): pl.pallas_call(store, out_shape=tuple((jax.ShapeDtypeStruct(v.shape, f32)...  1.34 us

profile of v2, /device:TPU:1, one launch (start us, length us, event | category | flops | bytes accessed | tf_op | source)
XLA Modules:
  0.0 35.4 jit_solution(5940711106762222193)
XLA Ops:
  1.3 32.8 %shard_map.94 = (f32[2,2,256,256]{3,2,1,0:T(8,128)S(1)}, f32[4,8,16,256]{3,2,1,0:T(8,128)S(1)}, f32[2,256,256]{2,1,0:T(8,128)S(1)}) custom-call(s32[2]{0:T(128)} %bitcast.11, s32[1]{0:T(128)} %bitcast.7.count, f32[2,2,256,256]{3,2,1,0:T(8,128)} %obj_hbm.1, f32[4,8,16,256]{3,2,1,0:T(8,128)} %bitcast.9, f32[2,256,256]{2,1,0:T(8,128)} %probe_hbm.1, ...), custom_call_target="tpu_custom_call" | custom-call | tf_op jit(solution)/shard_map/pallas_call | solution.py:589
  34.1 1.3 %shard_map.95 = (f32[2,2,256,256]{3,2,1,0:T(8,128)}, f32[4,8,16,256]{3,2,1,0:T(8,128)}, f32[2,256,256]{2,1,0:T(8,128)}) custom-call(f32[2,2,256,256]{3,2,1,0:T(8,128)S(1)} %get-tuple-element.9.obj, f32[4,8,16,256]{3,2,1,0:T(8,128)S(1)} %get-tuple-element.10.probe, f32[2,256,256]{2,1,0:T(8,128)S(1)} %get-tuple-element.11.part), custom_call_target="tpu_custom_call" | custom-call | tf_op jit(solution)/shard_map/pallas_call | solution.py:604

commit v3 on v2

--- a/solution.py
+++ b/solution.py
@@ -89,8 +89,8 @@
     out_obj, out_probe, out_part,
     obj, prev, probe, probe_piece, amp, table,
     my_off, off,
-    ns_in, strip_mid, strip_edge, fold_far, far_mid, far_edge, msg_mid, msg_edge, got_mid, got_edge, z,
-    gmsg_mid, gmsg_edge, gs_mid, gs_edge, acc_mid, acc_edge, ns_out, ns_back,
+    strip_mid, strip_edge, inner_edge, ns_pack, ns_inner, fold_far, far_mid, far_edge, msg_mid, msg_edge, got_mid, got_edge, z,
+    gmsg_mid, gmsg_edge, gs_mid, gs_edge, pack_out, inner_out, pack_mid, pack_edge, in_mid, in_edge,
     buf1, buf2,
     local_sem, off_send, off_recv, ns_send, ns_recv, far_send, far_recv, msg_send, msg_recv,
     row_send, row_recv, col_send, col_recv, known,
@@ -195,6 +195,14 @@
             return jnp.where(first, re[:, :wide], swap(im[:, :wide]))
         return jnp.where(first, swap(re[:, tile - wide :]), im[:, tile - wide :])
 
+    def inner_of(value):
+        return jnp.where(first, value[:, wide:], value[:, :wide])
+
+    def unpack(head, tail, inner):
+        re = cat([jnp.where(first, head, inner[0]), jnp.where(first, inner[0], swap(tail))], 1)
+        im = cat([jnp.where(first, swap(head), inner[1]), jnp.where(first, inner[1], tail)], 1)
+        return re, im
+
     def ends(value):
         return cat([value[:HALO], value[tile - HALO :]], 0)
 
@@ -204,6 +212,8 @@
             value = pack((obj[s, 0], obj[s, 1]), side)
             strip_mid[side, s] = value[HALO : tile - HALO]
             strip_edge[side, s] = ends(value)
+        for k in range(2):
+            inner_edge[s, k] = inner_of(ends(obj[s, k]))
     fetches[3].wait()
     turn_rows = lax.rem(top + tile - HALO, tile)
     turn_cols = lax.rem(left + tile - HALO, tile)
@@ -227,15 +237,13 @@
         off[far] = jnp.full((2, 8, wide), HALO, jnp.int32)
 
     for s in range(2):
-        @pl.when(jnp.logical_not(has_south))
-        def _():
-            ns_in[s, :, :HALO, :] = jnp.zeros((2, HALO, tile), jnp.float32)
-            ns_back[s, :, HALO:, :] = jnp.zeros((2, HALO, tile), jnp.float32)
-
-        @pl.when(jnp.logical_not(has_north))
-        def _():
-            ns_in[s, :, HALO:, :] = jnp.zeros((2, HALO, tile), jnp.float32)
-            ns_back[s, :, :HALO, :] = jnp.zeros((2, HALO, tile), jnp.float32)
+        for phase, spans in ((0, ((has_south, slice(0, HALO)), (has_north, slice(HALO, wide)))),
+                             (1, ((has_north, slice(0, HALO)), (has_south, slice(HALO, wide))))):
+            for ok, span in spans:
+                @pl.when(jnp.logical_not(ok))
+                def _():
+                    ns_pack[phase, s, :, span, :] = jnp.zeros((2, HALO, wide), jnp.float32)
+                    ns_inner[phase, s, :, span, :] = jnp.zeros((2, HALO, wide), jnp.float32)
 
         @pl.when(jnp.logical_not(has_ahead))
         def _():
@@ -273,19 +281,24 @@
     off_near = Link(my_off, off.at[1 - near], off_send.at[0], off_recv.at[0], (row, partner), always, always)
     off_far = Link(my_off, off.at[1 - far], off_send.at[1], off_recv.at[1], (row, other), has_other, has_other)
 
-    def ns_links(phase, s):
-        if phase == 0:
-            src_up, src_down, dst = obj.at[s, :, up, :], obj.at[s, :, tile - HALO :, :], ns_in
-            to_up, to_down = (row - 1, has_north, has_south), (row + 1, has_south, has_north)
+    north, south = (row - 1, has_north, has_south), (row + 1, has_south, has_north)
+
+    def ns_links(phase, s, kind):
+        if kind == 0:
+            src = strip_edge.at[:, s] if phase == 0 else pack_out.at[s]
+            dst = ns_pack.at[phase, s]
         else:
-            src_up, src_down, dst = ns_out.at[s, :, up, :], ns_out.at[s, :, down, :], ns_back
-            to_up, to_down = (row + 1, has_south, has_north), (row - 1, has_north, has_south)
-        return [
-            Link(src, dst.at[s, :, span, :], ns_send.at[phase, s, k], ns_recv.at[phase, s, k], (to[0], col), to[1], to[2])
-            for k, (src, span, to) in enumerate(((src_up, up, to_up), (src_down, down, to_down)))
-        ]
-
-    ns = [[ns_links(phase, s) for s in range(2)] for phase in range(2)]
+            src = (inner_edge if phase == 0 else inner_out).at[s]
+            dst = ns_inner.at[phase, s]
+        made = []
+        for k, (span, to) in enumerate(((up, south if phase else north), (down, north if phase else south))):
+            sem = 2 * kind + k
+            made.append(Link(src.at[:, span, :], dst.at[:, span, :], ns_send.at[phase, s, sem], ns_recv.at[phase, s, sem],
+                             (to[0], col), to[1], to[2]))
+        return made
+
+    PACK, INNER = 0, 1
+    ns = [[[ns_links(phase, s, kind) for kind in range(2)] for s in range(2)] for phase in range(2)]
     MID, EDGE = 0, 1
     far_link = [
         [
@@ -341,9 +354,12 @@
     off_far.start()
     row_down[0].start()
     for s in range(2):
-        for link in ns[0][s]:
+        for link in ns[0][s][PACK]:
             link.start()
         far_link[s][MID].start()
+    for s in range(2):
+        for link in ns[0][s][INNER]:
+            link.start()
     for bit in bits:
         greet(known.at[0], row, flip(col, bit))
 
@@ -355,14 +371,11 @@
     take_own = jnp.where(near == 0, near_left - HALO, HALO - near_left) > 0
 
     def fold(s):
-        for link in ns[0][s]:
+        for link in ns[0][s][PACK]:
             link.arrive()
-        packs = [pack((ns_in[s, 0], ns_in[s, 1]), slot) for slot in range(2)]
-        far_pack = jnp.where(far == 0, packs[0], packs[1])
-        near_pack = jnp.where(near == 0, packs[0], packs[1])
-        fold_far[s] = jnp.where(turned(line, far_top), far_pack, strip_edge[far, s])
+        fold_far[s] = jnp.where(turned(line, far_top), ns_pack[0, s, far], strip_edge[far, s])
         far_link[s][EDGE].start()
-        msg_edge[s] = jnp.where(turned(line, near_top), near_pack, strip_edge[near, s])
+        msg_edge[s] = jnp.where(turned(line, near_top), ns_pack[0, s, near], strip_edge[near, s])
 
     def forward_mid(s):
         far_link[s][MID].arrive()
@@ -393,42 +406,50 @@
                 greet(known.at[wait_round + 1], row, flip(col, again))
 
     def assemble(s):
-        from_east, from_west = lane < left - HALO, lane >= left + HALO
-
-        def columns(base, strip):
-            turned_strip = swap(strip)
-            for k in range(2):
-                re_like, im_like = (strip, turned_strip) if k == 0 else (turned_strip, strip)
-                head = jnp.where(from_east, re_like, base[k][:, :wide])
-                tail = jnp.where(from_west, im_like, base[k][:, tile - wide :])
-                yield cat([head, base[k][:, wide : tile - wide], tail], 1) if tile > 2 * wide else cat([head, tail], 1)
+        from_east, from_west = lane64 < left - HALO, lane64 >= left
 
         msg_link[s][MID].arrive()
-        for k, value in enumerate(columns([obj[s, p, HALO : tile - HALO, :] for p in range(2)], got_mid[s])):
+        packs = [jnp.where(take, got_mid[s], strip_mid[side, s]) for side, take in enumerate((from_east, from_west))]
+        inner = [inner_of(obj[s, k, HALO : tile - HALO, :]) for k in range(2)]
+        for k, value in enumerate(unpack(*packs, inner)):
             z[s, k, HALO : tile - HALO, :] = value
+        for link in ns[0][s][INNER]:
+            link.arrive()
+        away = turned(line, top)
+        inner = [jnp.where(away, ns_inner[0, s, k], inner_edge[s, k]) for k in range(2)]
+        packs = [jnp.where(away, ns_pack[0, s, side], strip_edge[side, s]) for side in range(2)]
         msg_link[s][EDGE].arrive()
-        base = [jnp.where(turned(line, top), ns_in[s, p], ends(obj[s, p])) for p in range(2)]
-        for k, value in enumerate(columns(base, got_edge[s])):
+        packs = [jnp.where(take, got_edge[s], packs[side]) for side, take in enumerate((from_east, from_west))]
+        for k, value in enumerate(unpack(*packs, inner)):
             z[s, k, :HALO, :] = value[:HALO]
             z[s, k, tile - HALO :, :] = value[HALO:]
 
     def back(s, gre, gim):
-        east = jnp.where(lane64 < left - HALO, pack((gre, gim), 0), 0.0)
-        west = jnp.where(lane64 >= left, pack((gre, gim), 1), 0.0)
-        value = jnp.where(left > HALO, east, west)
+        leaves = lane64 < left - HALO, lane64 >= left
+        packs = [pack((gre, gim), side) for side in range(2)]
+        out = [jnp.where(leave, value, 0.0) for leave, value in zip(leaves, packs)]
+        value = jnp.where(left > HALO, out[0], out[1])
         gmsg_edge[s] = ends(value)
         gmsg_link[s][EDGE].start()
         gmsg_mid[s] = value[HALO : tile - HALO]
-        gmsg_link[s][MID].start()
+        if s == 0:
+            gmsg_link[1][MID].start()
+            gmsg_link[0][MID].start()
         away = turned(line, top)
-        lanes = lax.broadcasted_iota(jnp.int32, (1, tile), 1)
-        stay = jnp.logical_not((lanes < left - HALO) | (lanes >= left + tile - HALO))
-        for k, grad in enumerate((gre, gim)):
-            grad = jnp.where(stay, grad, 0.0)
-            acc_mid[s, k] = grad[HALO : tile - HALO]
-            edge = ends(grad)
-            acc_edge[s, k] = jnp.where(away, 0.0, edge)
-            ns_out[s, k] = jnp.where(away, edge, 0.0)
+        inner = [inner_of(grad) for grad in (gre, gim)]
+        for k in range(2):
+            edge = ends(inner[k])
+            inner_out[s, k] = jnp.where(away, edge, 0.0)
+            in_edge[s, k] = jnp.where(away, 0.0, edge)
+        for link in ns[1][s][INNER]:
+            link.start()
+        for k in range(2):
+            in_mid[s, k] = inner[k][HALO : tile - HALO]
+            stay = jnp.where(leaves[k], 0.0, packs[k])
+            pack_mid[s, k] = stay[HALO : tile - HALO]
+            edge = ends(stay)
+            pack_out[s, k] = jnp.where(away, edge, 0.0)
+            pack_edge[s, k] = jnp.where(away, 0.0, edge)
 
     if len(row_bits) > 1:
         add_rows(len(row_bits) - 1)
@@ -466,20 +487,15 @@
     ur, ui = sandwich(xr * br + xi * bi, xi * br - xr * bi, table, 1, True)
     back(0, ur * pr + ui * pi, ui * pr - ur * pi)
 
-    for s in (1,):
-        for piece in (EDGE, MID):
-            gmsg_link[s][piece].arrive()
-            pass_link[s][piece].start()
-
+    def relay(s, piece):
+        gmsg_link[s][piece].arrive()
+        pass_link[s][piece].start()
+
+    relay(1, EDGE)
     for copy in ag_cols:
         copy.wait_recv()
     spread_rows(0)
-
-    for s in (0,):
-        for piece in (EDGE, MID):
-            gmsg_link[s][piece].arrive()
-            pass_link[s][piece].start()
-
+    relay(0, EDGE)
     home_rows = lax.rem(tile + HALO - top, tile)
     home_cols = lax.rem(tile + HALO - left, tile)
     out_part[0] = pltpu.roll(pltpu.roll(ur * ar + ui * ai, home_rows, 0), home_cols, 1)
@@ -488,42 +504,40 @@
     head_off, tail_off = off[0], off[1]
     accept = (head_off[1, :1] > HALO, tail_off[1, :1] < HALO)
     corner = (head_off[0, :1], tail_off[0, :1])
-    span = (slice(0, wide), slice(tile - wide, tile))
-
-    def parts_of(slot, strip):
-        if slot == 0:
-            return jnp.where(first, strip, 0.0), jnp.where(first, swap(strip), 0.0)
-        return jnp.where(first, 0.0, swap(strip)), jnp.where(first, 0.0, strip)
 
     def collect_edge(s):
         pass_link[s][EDGE].arrive()
-        for slot in range(2):
-            strip = jnp.where(accept[slot], gs_edge[slot, s], 0.0)
-            moves = turned(line, corner[slot])
-            for dst, kept in ((ns_out, jnp.where(moves, strip, 0.0)), (acc_edge, jnp.where(moves, 0.0, strip))):
-                for k, value in enumerate(parts_of(slot, kept)):
-                    dst[s, k, :, span[slot]] += value
-        for link in ns[1][s]:
+        for side in range(2):
+            strip = jnp.where(accept[side], gs_edge[side, s], 0.0)
+            moves = turned(line, corner[side])
+            pack_out[s, side] += jnp.where(moves, strip, 0.0)
+            pack_edge[s, side] += jnp.where(moves, 0.0, strip)
+        for link in ns[1][s][PACK]:
             link.start()
 
     def collect_mid(s):
         pass_link[s][MID].arrive()
-        for slot in range(2):
-            strip = jnp.where(accept[slot], gs_mid[slot, s], 0.0)
-            for k, value in enumerate(parts_of(slot, strip)):
-                acc_mid[s, k, :, span[slot]] += value
-        for k in range(2):
-            out_obj[s, k, HALO : tile - HALO, :] = obj[s, k, HALO : tile - HALO, :] - OBJ_RATE * acc_mid[s, k]
+        packs = [
+            strip_mid[side, s] - OBJ_RATE * (pack_mid[s, side] + jnp.where(accept[side], gs_mid[side, s], 0.0))
+            for side in range(2)
+        ]
+        inner = [inner_of(obj[s, k, HALO : tile - HALO, :]) - OBJ_RATE * in_mid[s, k] for k in range(2)]
+        for k, value in enumerate(unpack(*packs, inner)):
+            out_obj[s, k, HALO : tile - HALO, :] = value
 
     def finish_edge(s):
-        for link in ns[1][s]:
-            link.arrive()
-        for k in range(2):
-            value = ends(obj[s, k]) - OBJ_RATE * (acc_edge[s, k] + ns_back[s, k])
+        for kind in (INNER, PACK):
+            for link in ns[1][s][kind]:
+                link.arrive()
+        packs = [strip_edge[side, s] - OBJ_RATE * (pack_edge[s, side] + ns_pack[1, s, side]) for side in range(2)]
+        inner = [inner_edge[s, k] - OBJ_RATE * (in_edge[s, k] + ns_inner[1, s, k]) for k in range(2)]
+        for k, value in enumerate(unpack(*packs, inner)):
             out_obj[s, k, :HALO, :] = value[:HALO]
             out_obj[s, k, tile - HALO :, :] = value[HALO:]
 
     collect_edge(1)
+    relay(1, MID)
+    relay(0, MID)
     collect_edge(0)
     for held in range(1, rows):
         spread_rows(held)
@@ -536,7 +550,7 @@
     off_far.sent()
     for s in range(2):
         for phase in range(2):
-            for link in ns[phase][s]:
+            for link in ns[phase][s][PACK] + ns[phase][s][INNER]:
                 link.sent()
         for piece in range(2):
             for group in (far_link, msg_link, gmsg_link, pass_link):
@@ -559,7 +573,7 @@
 def shards(rows, cols, objects, probe, prev_partial, offsets, counts, amplitudes):
     tile = objects.shape[2]
     win = probe.shape[-1]
-    assert tile == win and cols % 2 == 0
+    assert tile == win == 4 * HALO and cols % 2 == 0
     piece = (2 * win) // (rows * cols)
     split_shape = (rows, cols, piece, win)
     table = jnp.asarray(operator_table(win))
@@ -574,13 +588,14 @@
         V(2, 2, tile, tile), V(*split_shape), V(2, win, win), V(piece, win), V(win, win),
         pltpu.VMEM(table.shape, jnp.bfloat16),
         pltpu.VMEM((2, 8, wide), jnp.int32), pltpu.VMEM((2, 2, 8, wide), jnp.int32),
-        V(2, 2, wide, tile), V(2, 2, mid, wide), V(2, 2, wide, wide), V(2, wide, wide),
+        V(2, 2, mid, wide), V(2, 2, wide, wide), V(2, 2, wide, wide), V(2, 2, 2, wide, wide), V(2, 2, 2, wide, wide),
+        V(2, wide, wide),
         V(2, mid, wide), V(2, wide, wide), V(2, mid, wide), V(2, wide, wide), V(2, mid, wide), V(2, wide, wide),
         V(2, 2, tile, tile),
         V(2, mid, wide), V(2, wide, wide), V(2, 2, mid, wide), V(2, 2, wide, wide),
-        V(2, 2, mid, tile), V(2, 2, wide, tile), V(2, 2, wide, tile), V(2, 2, wide, tile),
+        V(2, 2, wide, wide), V(2, 2, wide, wide), V(2, 2, mid, wide), V(2, 2, wide, wide), V(2, 2, mid, wide), V(2, 2, wide, wide),
         V(max(rows - 1, 1), cols, piece, win), V(max(cols - 1, 1), piece, win),
-        dma((7,)), dma((2,)), dma((2,)), dma((2, 2, 2)), dma((2, 2, 2)),
+        dma((7,)), dma((2,)), dma((2,)), dma((2, 2, 4)), dma((2, 2, 4)),
         dma((2, 2, 2)), dma((2, 2, 2)), dma((2, 2, 2)), dma((2, 2, 2)),
         dma((2, max(rows - 1, 1))), dma((2, max(rows - 1, 1))),
         dma((2, max(cols - 1, 1))), dma((2, max(cols - 1, 1))),

time: 35.8 us -> 34.6 us (0.966)
  Pallas kernels: 34.1 us -> 33.1 us
    pallas_call x1, Pallas kernels: 32.8 us -> 31.8 us  [shards(): pl.pallas_call(functools.partial(kernel, rows, cols), out_shape=(pltpu.VM...]
where the time goes in v3:
time: 34.6 us; the launch traced here: 34.4 us
  Pallas kernels  33.1 us (96%)
  between operations  1.29 us (4%)
    pallas_call x1, Pallas kernels, shards(): pl.pallas_call(functools.partial(kernel, rows, cols), out_shape=(pltpu.VM...  31.8 us
    pallas_call x1, Pallas kernels, shards(): pl.pallas_call(store, out_shape=tuple((jax.ShapeDtypeStruct(v.shape, f32)...  1.34 us

profile of v3, /device:TPU:1, one launch (start us, length us, event | category | flops | bytes accessed | tf_op | source)
XLA Modules:
  0.0 34.4 jit_solution(8929766955231336690)
XLA Ops:
  1.3 31.8 %shard_map.94 = (f32[2,2,256,256]{3,2,1,0:T(8,128)S(1)}, f32[4,8,16,256]{3,2,1,0:T(8,128)S(1)}, f32[2,256,256]{2,1,0:T(8,128)S(1)}) custom-call(s32[2]{0:T(128)} %bitcast.11, s32[1]{0:T(128)} %bitcast.7.count, f32[2,2,256,256]{3,2,1,0:T(8,128)} %obj_hbm.1, f32[4,8,16,256]{3,2,1,0:T(8,128)} %bitcast.9, f32[2,256,256]{2,1,0:T(8,128)} %probe_hbm.1, ...), custom_call_target="tpu_custom_call" | custom-call | tf_op jit(solution)/shard_map/pallas_call | solution.py:604
  33.1 1.3 %shard_map.95 = (f32[2,2,256,256]{3,2,1,0:T(8,128)}, f32[4,8,16,256]{3,2,1,0:T(8,128)}, f32[2,256,256]{2,1,0:T(8,128)}) custom-call(f32[2,2,256,256]{3,2,1,0:T(8,128)S(1)} %get-tuple-element.9.obj, f32[4,8,16,256]{3,2,1,0:T(8,128)S(1)} %get-tuple-element.10.probe, f32[2,256,256]{2,1,0:T(8,128)S(1)} %get-tuple-element.11.part), custom_call_target="tpu_custom_call" | custom-call | tf_op jit(solution)/shard_map/pallas_call | solution.py:619

commit v4 on v3

--- a/solution.py
+++ b/solution.py
@@ -85,14 +85,14 @@
 
 
 def kernel(
-    rows, cols, offs, count, obj_hbm, prev_hbm, probe_hbm, probe_k_hbm, amp_hbm, table_hbm,
+    rows, cols, offs_hbm, count_hbm, obj_hbm, prev_hbm, probe_hbm, probe_k_hbm, amp_hbm, table_hbm,
     out_obj, out_probe, out_part,
     obj, prev, probe, probe_piece, amp, table,
     my_off, off,
     strip_mid, strip_edge, inner_edge, ns_pack, ns_inner, fold_far, far_mid, far_edge, msg_mid, msg_edge, got_mid, got_edge, z,
     gmsg_mid, gmsg_edge, gs_mid, gs_edge, pack_out, inner_out, pack_mid, pack_edge, in_mid, in_edge,
     buf1, buf2,
-    local_sem, off_send, off_recv, ns_send, ns_recv, far_send, far_recv, msg_send, msg_recv,
+    offs, count, local_sem, off_send, off_recv, ns_send, ns_recv, far_send, far_recv, msg_send, msg_recv,
     row_send, row_recv, col_send, col_recv, known,
 ):
     tile = obj.shape[2]
@@ -149,11 +149,11 @@
         for k, (src, dst) in enumerate(
             ((obj_hbm.at[0], obj.at[0]), (obj_hbm.at[1], obj.at[1]), (prev_hbm, prev),
              (probe_hbm, probe), (probe_k_hbm.at[slot, col], probe_piece),
-             (table_hbm, table), (amp_hbm, amp))
+             (table_hbm, table), (amp_hbm, amp), (offs_hbm, offs), (count_hbm, count))
         )
     ]
-    for fetch in fetches:
-        fetch.start()
+    for k in (7, 0, 1, 2):
+        fetches[k].start()
 
     barrier = pltpu.get_barrier_semaphore()
 
@@ -174,6 +174,7 @@
         greet(barrier, row, flip(col, bit))
         expected = expected + 1
 
+    fetches[7].wait()
     top, left = offs[0], offs[1]
     my_off[0] = jnp.zeros((8, wide), jnp.int32) + top
     my_off[1] = jnp.zeros((8, wide), jnp.int32) + left
@@ -205,55 +206,6 @@
 
     def ends(value):
         return cat([value[:HALO], value[tile - HALO :]], 0)
-
-    for s in range(2):
-        fetches[s].wait()
-        for side in range(2):
-            value = pack((obj[s, 0], obj[s, 1]), side)
-            strip_mid[side, s] = value[HALO : tile - HALO]
-            strip_edge[side, s] = ends(value)
-        for k in range(2):
-            inner_edge[s, k] = inner_of(ends(obj[s, k]))
-    fetches[3].wait()
-    turn_rows = lax.rem(top + tile - HALO, tile)
-    turn_cols = lax.rem(left + tile - HALO, tile)
-    for k in range(2):
-        probe[k] = pltpu.roll(pltpu.roll(probe[k], turn_rows, 0), turn_cols, 1)
-
-    fetches[6].wait()
-    count_half = tile // 2
-
-    def order(axis):
-        target = lax.broadcasted_iota(jnp.int32, (tile, tile), axis)
-        source = lax.broadcasted_iota(jnp.int32, (tile, tile), 1 - axis)
-        target = jnp.where(target < count_half, 2 * target, 2 * (target - count_half) + 1)
-        return (source == target).astype(jnp.float32).astype(jnp.bfloat16)
-
-    ordered = dot(cat([order(0), order(0)], 1), cat(split(amp[...]), 0))
-    amp[...] = dot(cat(split(ordered), 1), cat([order(1), order(1)], 0))
-
-    @pl.when(jnp.logical_not(has_other))
-    def _():
-        off[far] = jnp.full((2, 8, wide), HALO, jnp.int32)
-
-    for s in range(2):
-        for phase, spans in ((0, ((has_south, slice(0, HALO)), (has_north, slice(HALO, wide)))),
-                             (1, ((has_north, slice(0, HALO)), (has_south, slice(HALO, wide))))):
-            for ok, span in spans:
-                @pl.when(jnp.logical_not(ok))
-                def _():
-                    ns_pack[phase, s, :, span, :] = jnp.zeros((2, HALO, wide), jnp.float32)
-                    ns_inner[phase, s, :, span, :] = jnp.zeros((2, HALO, wide), jnp.float32)
-
-        @pl.when(jnp.logical_not(has_ahead))
-        def _():
-            far_mid[s] = jnp.zeros((mid_rows, wide), jnp.float32)
-            far_edge[s] = jnp.zeros((wide, wide), jnp.float32)
-
-        @pl.when(jnp.logical_not(has_behind))
-        def _():
-            gs_mid[far, s] = jnp.zeros((mid_rows, wide), jnp.float32)
-            gs_edge[far, s] = jnp.zeros((wide, wide), jnp.float32)
 
     class Link:
         def __init__(self, src, dst, send_sem, recv_sem, device, ok, inbound):
@@ -299,35 +251,32 @@
 
     PACK, INNER = 0, 1
     ns = [[[ns_links(phase, s, kind) for kind in range(2)] for s in range(2)] for phase in range(2)]
-    MID, EDGE = 0, 1
-    far_link = [
-        [
-            Link(strip_mid.at[far, s], far_mid.at[s], far_send.at[0, s, 0], far_recv.at[0, s, 0], (row, behind), has_behind, has_ahead),
-            Link(fold_far.at[s], far_edge.at[s], far_send.at[0, s, 1], far_recv.at[0, s, 1], (row, behind), has_behind, has_ahead),
-        ]
-        for s in range(2)
-    ]
-    msg_link = [
-        [
-            Link(msg_mid.at[s], got_mid.at[s], msg_send.at[0, s, 0], msg_recv.at[0, s, 0], (row, partner), always, always),
-            Link(msg_edge.at[s], got_edge.at[s], msg_send.at[0, s, 1], msg_recv.at[0, s, 1], (row, partner), always, always),
-        ]
-        for s in range(2)
-    ]
-    gmsg_link = [
-        [
-            Link(gmsg_mid.at[s], gs_mid.at[1 - near, s], msg_send.at[1, s, 0], msg_recv.at[1, s, 0], (row, partner), always, always),
-            Link(gmsg_edge.at[s], gs_edge.at[1 - near, s], msg_send.at[1, s, 1], msg_recv.at[1, s, 1], (row, partner), always, always),
-        ]
-        for s in range(2)
-    ]
-    pass_link = [
-        [
-            Link(gs_mid.at[near, s], gs_mid.at[far, s], far_send.at[1, s, 0], far_recv.at[1, s, 0], (row, ahead), has_ahead, has_behind),
-            Link(gs_edge.at[near, s], gs_edge.at[far, s], far_send.at[1, s, 1], far_recv.at[1, s, 1], (row, ahead), has_ahead, has_behind),
-        ]
-        for s in range(2)
-    ]
+    MID, EDGE = (0, 1), (2, 3)
+    halves_of = (slice(0, HALO), slice(HALO, wide))
+
+    def chunks(make):
+        return [[make(s, p, p // 2, halves_of[p % 2]) for p in range(4)] for s in range(2)]
+
+    far_link = chunks(lambda s, p, b, rows_: Link(
+        fold_far.at[s, rows_] if b else strip_mid.at[far, s, rows_], (far_mid, far_edge)[b].at[s, rows_],
+        far_send.at[0, s, p], far_recv.at[0, s, p], (row, behind), has_behind, has_ahead))
+    msg_link = chunks(lambda s, p, b, rows_: Link(
+        (msg_mid, msg_edge)[b].at[s, rows_], (got_mid, got_edge)[b].at[s, rows_],
+        msg_send.at[0, s, p], msg_recv.at[0, s, p], (row, partner), always, always))
+    gmsg_link = chunks(lambda s, p, b, rows_: Link(
+        (gmsg_mid, gmsg_edge)[b].at[s, rows_], (gs_mid, gs_edge)[b].at[1 - near, s, rows_],
+        msg_send.at[1, s, p], msg_recv.at[1, s, p], (row, partner), always, always))
+    pass_link = chunks(lambda s, p, b, rows_: Link(
+        (gs_mid, gs_edge)[b].at[near, s, rows_], (gs_mid, gs_edge)[b].at[far, s, rows_],
+        far_send.at[1, s, p], far_recv.at[1, s, p], (row, ahead), has_ahead, has_behind))
+
+    def start(links, pieces):
+        for p in pieces:
+            links[p].start()
+
+    def arrive(links, pieces):
+        for p in pieces:
+            links[p].arrive()
 
     def add_rows(k):
         keep, count_rows, landing = row_keep[k]
@@ -347,21 +296,76 @@
                 recv_sem=col_recv.at[stage, t - 1], device_id=(row, peer), device_id_type=MESH))
         return made
 
-    fetches[2].wait()
+    def pack_slice(s):
+        fetches[s].wait()
+        for side in range(2):
+            value = pack((obj[s, 0], obj[s, 1]), side)
+            strip_mid[side, s] = value[HALO : tile - HALO]
+            strip_edge[side, s] = ends(value)
+
+    pack_slice(0)
     pl.semaphore_wait(barrier, expected)
-
     off_near.start()
     off_far.start()
+    for link in ns[0][0][PACK]:
+        link.start()
+    start(far_link[0], MID)
+    pack_slice(1)
+    for link in ns[0][1][PACK]:
+        link.start()
+    start(far_link[1], MID)
+    fetches[2].wait()
     row_down[0].start()
     for s in range(2):
-        for link in ns[0][s][PACK]:
-            link.start()
-        far_link[s][MID].start()
-    for s in range(2):
+        for k in range(2):
+            inner_edge[s, k] = inner_of(ends(obj[s, k]))
         for link in ns[0][s][INNER]:
             link.start()
     for bit in bits:
         greet(known.at[0], row, flip(col, bit))
+    for k in (3, 4, 5, 6, 8):
+        fetches[k].start()
+
+    @pl.when(jnp.logical_not(has_other))
+    def _():
+        off[far] = jnp.full((2, 8, wide), HALO, jnp.int32)
+
+    for s in range(2):
+        for phase, spans in ((0, ((has_south, slice(0, HALO)), (has_north, slice(HALO, wide)))),
+                             (1, ((has_north, slice(0, HALO)), (has_south, slice(HALO, wide))))):
+            for ok, span in spans:
+                @pl.when(jnp.logical_not(ok))
+                def _():
+                    ns_pack[phase, s, :, span, :] = jnp.zeros((2, HALO, wide), jnp.float32)
+                    ns_inner[phase, s, :, span, :] = jnp.zeros((2, HALO, wide), jnp.float32)
+
+        @pl.when(jnp.logical_not(has_ahead))
+        def _():
+            far_mid[s] = jnp.zeros((mid_rows, wide), jnp.float32)
+            far_edge[s] = jnp.zeros((wide, wide), jnp.float32)
+
+        @pl.when(jnp.logical_not(has_behind))
+        def _():
+            gs_mid[far, s] = jnp.zeros((mid_rows, wide), jnp.float32)
+            gs_edge[far, s] = jnp.zeros((wide, wide), jnp.float32)
+
+    fetches[3].wait()
+    turn_rows = lax.rem(top + tile - HALO, tile)
+    turn_cols = lax.rem(left + tile - HALO, tile)
+    for k in range(2):
+        probe[k] = pltpu.roll(pltpu.roll(probe[k], turn_rows, 0), turn_cols, 1)
+
+    fetches[6].wait()
+    count_half = tile // 2
+
+    def order(axis):
+        target = lax.broadcasted_iota(jnp.int32, (tile, tile), axis)
+        source = lax.broadcasted_iota(jnp.int32, (tile, tile), 1 - axis)
+        target = jnp.where(target < count_half, 2 * target, 2 * (target - count_half) + 1)
+        return (source == target).astype(jnp.float32).astype(jnp.bfloat16)
+
+    ordered = dot(cat([order(0), order(0)], 1), cat(split(amp[...]), 0))
+    amp[...] = dot(cat(split(ordered), 1), cat([order(1), order(1)], 0))
 
     off_near.arrive()
     off_far.arrive()
@@ -371,21 +375,24 @@
     take_own = jnp.where(near == 0, near_left - HALO, HALO - near_left) > 0
 
     def fold(s):
-        for link in ns[0][s][PACK]:
-            link.arrive()
-        fold_far[s] = jnp.where(turned(line, far_top), ns_pack[0, s, far], strip_edge[far, s])
-        far_link[s][EDGE].start()
-        msg_edge[s] = jnp.where(turned(line, near_top), ns_pack[0, s, near], strip_edge[near, s])
+        for h, rows_ in enumerate(halves_of):
+            ns[0][s][PACK][h].arrive()
+            fold_far[s, rows_] = jnp.where(turned(line[rows_], far_top), ns_pack[0, s, far, rows_], strip_edge[far, s, rows_])
+            far_link[s][EDGE[h]].start()
+        for rows_ in halves_of:
+            msg_edge[s, rows_] = jnp.where(turned(line[rows_], near_top), ns_pack[0, s, near, rows_], strip_edge[near, s, rows_])
 
     def forward_mid(s):
-        far_link[s][MID].arrive()
-        msg_mid[s] = jnp.where(take_own, strip_mid[near, s], far_mid[s])
-        msg_link[s][MID].start()
+        for p, rows_ in zip(MID, halves_of):
+            far_link[s][p].arrive()
+            msg_mid[s, rows_] = jnp.where(take_own, strip_mid[near, s, rows_], far_mid[s, rows_])
+            msg_link[s][p].start()
 
     def forward_edge(s):
-        far_link[s][EDGE].arrive()
-        msg_edge[s] = jnp.where(take_own, msg_edge[s], far_edge[s])
-        msg_link[s][EDGE].start()
+        for p, rows_ in zip(EDGE, halves_of):
+            far_link[s][p].arrive()
+            msg_edge[s, rows_] = jnp.where(take_own, msg_edge[s, rows_], far_edge[s, rows_])
+            msg_link[s][p].start()
 
     add_rows(0)
     for k in range(1, len(row_bits)):
@@ -408,7 +415,7 @@
     def assemble(s):
         from_east, from_west = lane64 < left - HALO, lane64 >= left
 
-        msg_link[s][MID].arrive()
+        arrive(msg_link[s], MID)
         packs = [jnp.where(take, got_mid[s], strip_mid[side, s]) for side, take in enumerate((from_east, from_west))]
         inner = [inner_of(obj[s, k, HALO : tile - HALO, :]) for k in range(2)]
         for k, value in enumerate(unpack(*packs, inner)):
@@ -418,7 +425,7 @@
         away = turned(line, top)
         inner = [jnp.where(away, ns_inner[0, s, k], inner_edge[s, k]) for k in range(2)]
         packs = [jnp.where(away, ns_pack[0, s, side], strip_edge[side, s]) for side in range(2)]
-        msg_link[s][EDGE].arrive()
+        arrive(msg_link[s], EDGE)
         packs = [jnp.where(take, got_edge[s], packs[side]) for side, take in enumerate((from_east, from_west))]
         for k, value in enumerate(unpack(*packs, inner)):
             z[s, k, :HALO, :] = value[:HALO]
@@ -430,11 +437,11 @@
         out = [jnp.where(leave, value, 0.0) for leave, value in zip(leaves, packs)]
         value = jnp.where(left > HALO, out[0], out[1])
         gmsg_edge[s] = ends(value)
-        gmsg_link[s][EDGE].start()
+        start(gmsg_link[s], EDGE)
         gmsg_mid[s] = value[HALO : tile - HALO]
         if s == 0:
-            gmsg_link[1][MID].start()
-            gmsg_link[0][MID].start()
+            start(gmsg_link[1], MID)
+            start(gmsg_link[0], MID)
         away = turned(line, top)
         inner = [inner_of(grad) for grad in (gre, gim)]
         for k in range(2):
@@ -466,6 +473,7 @@
     assemble(1)
     br, bi = z[1, 0], z[1, 1]
     wr, wi = sandwich(vr * br - vi * bi, vr * bi + vi * br, table, 0, False)
+    fetches[8].wait()
     live = jnp.where(count[0] > 0, 2.0, 0.0)
     scale = live - (live * amp[...]) * lax.rsqrt(wr * wr + wi * wi + 1.0)
     xr, xi = sandwich(scale * wr, scale * wi, table, 0, True)
@@ -487,9 +495,10 @@
     ur, ui = sandwich(xr * br + xi * bi, xi * br - xr * bi, table, 1, True)
     back(0, ur * pr + ui * pi, ui * pr - ur * pi)
 
-    def relay(s, piece):
-        gmsg_link[s][piece].arrive()
-        pass_link[s][piece].start()
+    def relay(s, pieces):
+        for p in pieces:
+            gmsg_link[s][p].arrive()
+            pass_link[s][p].start()
 
     relay(1, EDGE)
     for copy in ag_cols:
@@ -506,17 +515,20 @@
     corner = (head_off[0, :1], tail_off[0, :1])
 
     def collect_edge(s):
-        pass_link[s][EDGE].arrive()
-        for side in range(2):
-            strip = jnp.where(accept[side], gs_edge[side, s], 0.0)
-            moves = turned(line, corner[side])
-            pack_out[s, side] += jnp.where(moves, strip, 0.0)
-            pack_edge[s, side] += jnp.where(moves, 0.0, strip)
-        for link in ns[1][s][PACK]:
-            link.start()
+        for h, rows_ in enumerate(halves_of):
+            pass_link[s][EDGE[h]].arrive()
+            kept = []
+            for side in range(2):
+                strip = jnp.where(accept[side], gs_edge[side, s, rows_], 0.0)
+                moves = turned(line[rows_], corner[side])
+                pack_out[s, side, rows_] += jnp.where(moves, strip, 0.0)
+                kept.append(jnp.where(moves, 0.0, strip))
+            ns[1][s][PACK][h].start()
+            for side in range(2):
+                pack_edge[s, side, rows_] += kept[side]
 
     def collect_mid(s):
-        pass_link[s][MID].arrive()
+        arrive(pass_link[s], MID)
         packs = [
             strip_mid[side, s] - OBJ_RATE * (pack_mid[s, side] + jnp.where(accept[side], gs_mid[side, s], 0.0))
             for side in range(2)
@@ -552,7 +564,7 @@
         for phase in range(2):
             for link in ns[phase][s][PACK] + ns[phase][s][INNER]:
                 link.sent()
-        for piece in range(2):
+        for piece in range(4):
             for group in (far_link, msg_link, gmsg_link, pass_link):
                 group[s][piece].sent()
     for copy in row_down + rs_cols + ag_cols + list(row_up.values()):
@@ -578,7 +590,6 @@
     split_shape = (rows, cols, piece, win)
     table = jnp.asarray(operator_table(win))
     f32 = jnp.float32
-    smem = pl.BlockSpec(memory_space=pltpu.SMEM)
     anyspace = pl.BlockSpec(memory_space=pl.ANY)
     vmem = pl.BlockSpec(memory_space=pltpu.VMEM)
     V = lambda *shape: pltpu.VMEM(shape, f32)
@@ -595,8 +606,8 @@
         V(2, mid, wide), V(2, wide, wide), V(2, 2, mid, wide), V(2, 2, wide, wide),
         V(2, 2, wide, wide), V(2, 2, wide, wide), V(2, 2, mid, wide), V(2, 2, wide, wide), V(2, 2, mid, wide), V(2, 2, wide, wide),
         V(max(rows - 1, 1), cols, piece, win), V(max(cols - 1, 1), piece, win),
-        dma((7,)), dma((2,)), dma((2,)), dma((2, 2, 4)), dma((2, 2, 4)),
-        dma((2, 2, 2)), dma((2, 2, 2)), dma((2, 2, 2)), dma((2, 2, 2)),
+        pltpu.SMEM((2,), jnp.int32), pltpu.SMEM((1,), jnp.int32), dma((9,)), dma((2,)), dma((2,)), dma((2, 2, 4)), dma((2, 2, 4)),
+        dma((2, 2, 4)), dma((2, 2, 4)), dma((2, 2, 4)), dma((2, 2, 4)),
         dma((2, max(rows - 1, 1))), dma((2, max(rows - 1, 1))),
         dma((2, max(cols - 1, 1))), dma((2, max(cols - 1, 1))),
         pltpu.SemaphoreType.REGULAR((max(cols.bit_length() - 2, 1),)),
@@ -606,7 +617,7 @@
         out_shape=(
             pltpu.VMEM(objects.shape, f32), pltpu.VMEM(split_shape, f32), pltpu.VMEM(probe.shape, f32),
         ),
-        in_specs=[smem, smem] + [anyspace] * 6,
+        in_specs=[anyspace] * 8,
         out_specs=(vmem, vmem, vmem),
         scratch_shapes=scratch,
         compiler_params=pltpu.CompilerParams(

time: 34.6 us -> 32.9 us (0.951)
  Pallas kernels: 33.1 us -> 31.2 us
    pallas_call x1, Pallas kernels: 31.8 us -> 29.9 us  [shards(): pl.pallas_call(functools.partial(kernel, rows, cols), out_shape=(pltpu.VM...]
where the time goes in v4:
time: 32.9 us; the launch traced here: 32.5 us
  Pallas kernels  31.2 us (95%)
  between operations  1.29 us (4%)
    pallas_call x1, Pallas kernels, shards(): pl.pallas_call(functools.partial(kernel, rows, cols), out_shape=(pltpu.VM...  29.9 us
    pallas_call x1, Pallas kernels, shards(): pl.pallas_call(store, out_shape=tuple((jax.ShapeDtypeStruct(v.shape, f32)...  1.34 us

profile of v4, /device:TPU:1, one launch (start us, length us, event | category | flops | bytes accessed | tf_op | source)
XLA Modules:
  0.0 32.5 jit_solution(7720750322412534045)
XLA Ops:
  1.3 29.9 %shard_map.94 = (f32[2,2,256,256]{3,2,1,0:T(8,128)S(1)}, f32[4,8,16,256]{3,2,1,0:T(8,128)S(1)}, f32[2,256,256]{2,1,0:T(8,128)S(1)}) custom-call(s32[2]{0:T(128)} %bitcast.11, s32[1]{0:T(128)} %bitcast.7.count_hbm, f32[2,2,256,256]{3,2,1,0:T(8,128)} %obj_hbm.1, f32[4,8,16,256]{3,2,1,0:T(8,128)} %bitcast.9, f32[2,256,256]{2,1,0:T(8,128)} %probe_hbm.1, ...), custom_call_target="tpu_custom_call" | custom-call | tf_op jit(solution)/shard_map/pallas_call | solution.py:615
  31.1 1.3 %shard_map.95 = (f32[2,2,256,256]{3,2,1,0:T(8,128)}, f32[4,8,16,256]{3,2,1,0:T(8,128)}, f32[2,256,256]{2,1,0:T(8,128)}) custom-call(f32[2,2,256,256]{3,2,1,0:T(8,128)S(1)} %get-tuple-element.9.obj, f32[4,8,16,256]{3,2,1,0:T(8,128)S(1)} %get-tuple-element.10.probe, f32[2,256,256]{2,1,0:T(8,128)S(1)} %get-tuple-element.11.part), custom_call_target="tpu_custom_call" | custom-call | tf_op jit(solution)/shard_map/pallas_call | solution.py:630

commit v5 on v4

--- a/solution.py
+++ b/solution.py
@@ -310,17 +310,12 @@
     for link in ns[0][0][PACK]:
         link.start()
     start(far_link[0], MID)
+    fetches[2].wait()
+    row_down[0].start()
     pack_slice(1)
     for link in ns[0][1][PACK]:
         link.start()
     start(far_link[1], MID)
-    fetches[2].wait()
-    row_down[0].start()
-    for s in range(2):
-        for k in range(2):
-            inner_edge[s, k] = inner_of(ends(obj[s, k]))
-        for link in ns[0][s][INNER]:
-            link.start()
     for bit in bits:
         greet(known.at[0], row, flip(col, bit))
     for k in (3, 4, 5, 6, 8):
@@ -349,24 +344,6 @@
             gs_mid[far, s] = jnp.zeros((mid_rows, wide), jnp.float32)
             gs_edge[far, s] = jnp.zeros((wide, wide), jnp.float32)
 
-    fetches[3].wait()
-    turn_rows = lax.rem(top + tile - HALO, tile)
-    turn_cols = lax.rem(left + tile - HALO, tile)
-    for k in range(2):
-        probe[k] = pltpu.roll(pltpu.roll(probe[k], turn_rows, 0), turn_cols, 1)
-
-    fetches[6].wait()
-    count_half = tile // 2
-
-    def order(axis):
-        target = lax.broadcasted_iota(jnp.int32, (tile, tile), axis)
-        source = lax.broadcasted_iota(jnp.int32, (tile, tile), 1 - axis)
-        target = jnp.where(target < count_half, 2 * target, 2 * (target - count_half) + 1)
-        return (source == target).astype(jnp.float32).astype(jnp.bfloat16)
-
-    ordered = dot(cat([order(0), order(0)], 1), cat(split(amp[...]), 0))
-    amp[...] = dot(cat(split(ordered), 1), cat([order(1), order(1)], 0))
-
     off_near.arrive()
     off_far.arrive()
     near_off, far_off = off[near], off[far]
@@ -399,10 +376,33 @@
         row_down[k].start()
         if k + 1 < len(row_bits):
             add_rows(k)
+    for s in range(2):
+        for k in range(2):
+            inner_edge[s, k] = inner_of(ends(obj[s, k]))
+        for link in ns[0][s][INNER]:
+            link.start()
     fold(0)
     forward_mid(0)
     fold(1)
     forward_mid(1)
+    fetches[3].wait()
+    turn_rows = lax.rem(top + tile - HALO, tile)
+    turn_cols = lax.rem(left + tile - HALO, tile)
+    for k in range(2):
+        probe[k] = pltpu.roll(pltpu.roll(probe[k], turn_rows, 0), turn_cols, 1)
+
+    fetches[6].wait()
+    count_half = tile // 2
+
+    def order(axis):
+        target = lax.broadcasted_iota(jnp.int32, (tile, tile), axis)
+        source = lax.broadcasted_iota(jnp.int32, (tile, tile), 1 - axis)
+        target = jnp.where(target < count_half, 2 * target, 2 * (target - count_half) + 1)
+        return (source == target).astype(jnp.float32).astype(jnp.bfloat16)
+
+    ordered = dot(cat([order(0), order(0)], 1), cat(split(amp[...]), 0))
+    amp[...] = dot(cat(split(ordered), 1), cat([order(1), order(1)], 0))
+
     forward_edge(0)
     forward_edge(1)
 
@@ -431,32 +431,40 @@
             z[s, k, :HALO, :] = value[:HALO]
             z[s, k, tile - HALO :, :] = value[HALO:]
 
-    def back(s, gre, gim):
+    def back(s, edge, middle):
         leaves = lane64 < left - HALO, lane64 >= left
-        packs = [pack((gre, gim), side) for side in range(2)]
-        out = [jnp.where(leave, value, 0.0) for leave, value in zip(leaves, packs)]
-        value = jnp.where(left > HALO, out[0], out[1])
-        gmsg_edge[s] = ends(value)
+        away = turned(line, top)
+
+        def strips(grad):
+            packs = [pack(grad, side) for side in range(2)]
+            out = [jnp.where(leave, value, 0.0) for leave, value in zip(leaves, packs)]
+            stay = [jnp.where(leave, 0.0, value) for leave, value in zip(leaves, packs)]
+            return jnp.where(left > HALO, out[0], out[1]), stay, [inner_of(part) for part in grad]
+
+        grad = edge()
+        gmsg_edge[s], stay, inner = strips(grad)
         start(gmsg_link[s], EDGE)
-        gmsg_mid[s] = value[HALO : tile - HALO]
+        for k in range(2):
+            inner_out[s, k] = jnp.where(away, inner[k], 0.0)
+            in_edge[s, k] = jnp.where(away, 0.0, inner[k])
+        for link in ns[1][s][INNER]:
+            link.start()
+        for k in range(2):
+            pack_out[s, k] = jnp.where(away, stay[k], 0.0)
+            pack_edge[s, k] = jnp.where(away, 0.0, stay[k])
+        gmsg_mid[s], stay, inner = strips(middle())
         if s == 0:
             start(gmsg_link[1], MID)
             start(gmsg_link[0], MID)
-        away = turned(line, top)
-        inner = [inner_of(grad) for grad in (gre, gim)]
         for k in range(2):
-            edge = ends(inner[k])
-            inner_out[s, k] = jnp.where(away, edge, 0.0)
-            in_edge[s, k] = jnp.where(away, 0.0, edge)
-        for link in ns[1][s][INNER]:
-            link.start()
-        for k in range(2):
-            in_mid[s, k] = inner[k][HALO : tile - HALO]
-            stay = jnp.where(leaves[k], 0.0, packs[k])
-            pack_mid[s, k] = stay[HALO : tile - HALO]
-            edge = ends(stay)
-            pack_out[s, k] = jnp.where(away, edge, 0.0)
-            pack_edge[s, k] = jnp.where(away, 0.0, edge)
+            in_mid[s, k] = inner[k]
+            pack_mid[s, k] = stay[k]
+
+    def inside(value):
+        return value[HALO : tile - HALO]
+
+    def product(ar, ai, br, bi):
+        return ar * br + ai * bi, ai * br - ar * bi
 
     if len(row_bits) > 1:
         add_rows(len(row_bits) - 1)
@@ -477,8 +485,9 @@
     live = jnp.where(count[0] > 0, 2.0, 0.0)
     scale = live - (live * amp[...]) * lax.rsqrt(wr * wr + wi * wi + 1.0)
     xr, xi = sandwich(scale * wr, scale * wi, table, 0, True)
-    back(1, xr * vr + xi * vi, xi * vr - xr * vi)
-
+    back(1, *[(lambda cut=cut: product(*[cut(v) for v in (xr, xi, vr, vi)])) for cut in (ends, inside)])
+
+    yr, yi = transform(*product(xr, xi, br, bi), table, 1, 0, True, True, True)
     for copy in rs_cols:
         copy.wait_recv()
     fetches[4].wait()
@@ -492,8 +501,14 @@
         copy.start()
 
 
-    ur, ui = sandwich(xr * br + xi * bi, xi * br - xr * bi, table, 1, True)
-    back(0, ur * pr + ui * pi, ui * pr - ur * pi)
+    u_parts = {}
+
+    def object_grad(cut):
+        u_parts[cut] = transform(cut(yr), cut(yi), table, 1, 1, True, True, True)
+        return product(*u_parts[cut], cut(pr), cut(pi))
+
+    back(0, lambda: object_grad(ends), lambda: object_grad(inside))
+    ur, ui = [cat([e[:HALO], m, e[HALO:]], 0) for e, m in zip(u_parts[ends], u_parts[inside])]
 
     def relay(s, pieces):
         for p in pieces:
@@ -551,11 +566,13 @@
     relay(1, MID)
     relay(0, MID)
     collect_edge(0)
-    for held in range(1, rows):
+    for held in range(1, rows // 2):
         spread_rows(held)
     collect_mid(1)
     collect_mid(0)
     finish_edge(1)
+    for held in range(rows // 2, rows):
+        spread_rows(held)
     finish_edge(0)
 
     off_near.sent()

time: 32.9 us -> 32.6 us (level)
  no operation moved by 1% of the time
where the time goes in v5:
time: 32.6 us; the launch traced here: 32.2 us
  Pallas kernels  30.9 us (95%)
  between operations  1.29 us (4%)
    pallas_call x1, Pallas kernels, shards(): pl.pallas_call(functools.partial(kernel, rows, cols), out_shape=(pltpu.VM...  29.5 us
    pallas_call x1, Pallas kernels, shards(): pl.pallas_call(store, out_shape=tuple((jax.ShapeDtypeStruct(v.shape, f32)...  1.34 us

profile of v5, /device:TPU:1, one launch (start us, length us, event | category | flops | bytes accessed | tf_op | source)
XLA Modules:
  0.0 32.2 jit_solution(9422256746138625336)
XLA Ops:
  1.3 29.5 %shard_map.94 = (f32[2,2,256,256]{3,2,1,0:T(8,128)S(1)}, f32[4,8,16,256]{3,2,1,0:T(8,128)S(1)}, f32[2,256,256]{2,1,0:T(8,128)S(1)}) custom-call(s32[2]{0:T(128)} %bitcast.11, s32[1]{0:T(128)} %bitcast.7.count_hbm, f32[2,2,256,256]{3,2,1,0:T(8,128)} %obj_hbm.1, f32[4,8,16,256]{3,2,1,0:T(8,128)} %bitcast.9, f32[2,256,256]{2,1,0:T(8,128)} %probe_hbm.1, ...), custom_call_target="tpu_custom_call" | custom-call | tf_op jit(solution)/shard_map/pallas_call | solution.py:632
  30.8 1.3 %shard_map.95 = (f32[2,2,256,256]{3,2,1,0:T(8,128)}, f32[4,8,16,256]{3,2,1,0:T(8,128)}, f32[2,256,256]{2,1,0:T(8,128)}) custom-call(f32[2,2,256,256]{3,2,1,0:T(8,128)S(1)} %get-tuple-element.9.obj, f32[4,8,16,256]{3,2,1,0:T(8,128)S(1)} %get-tuple-element.10.probe, f32[2,256,256]{2,1,0:T(8,128)S(1)} %get-tuple-element.11.part), custom_call_target="tpu_custom_call" | custom-call | tf_op jit(solution)/shard_map/pallas_call | solution.py:647

commit v6 on v5

--- a/solution.py
+++ b/solution.py
@@ -520,11 +520,6 @@
         copy.wait_recv()
     spread_rows(0)
     relay(0, EDGE)
-    home_rows = lax.rem(tile + HALO - top, tile)
-    home_cols = lax.rem(tile + HALO - left, tile)
-    out_part[0] = pltpu.roll(pltpu.roll(ur * ar + ui * ai, home_rows, 0), home_cols, 1)
-    out_part[1] = pltpu.roll(pltpu.roll(ui * ar - ur * ai, home_rows, 0), home_cols, 1)
-
     head_off, tail_off = off[0], off[1]
     accept = (head_off[1, :1] > HALO, tail_off[1, :1] < HALO)
     corner = (head_off[0, :1], tail_off[0, :1])
@@ -568,6 +563,11 @@
     collect_edge(0)
     for held in range(1, rows // 2):
         spread_rows(held)
+    home_rows = lax.rem(tile + HALO - top, tile)
+    home_cols = lax.rem(tile + HALO - left, tile)
+    out_part[0] = pltpu.roll(pltpu.roll(ur * ar + ui * ai, home_rows, 0), home_cols, 1)
+    out_part[1] = pltpu.roll(pltpu.roll(ui * ar - ur * ai, home_rows, 0), home_cols, 1)
+
     collect_mid(1)
     collect_mid(0)
     finish_edge(1)

time: 32.6 us -> 32.6 us (level)
  no operation moved by 1% of the time
where the time goes in v6:
time: 32.6 us; the launch traced here: 32.3 us
  Pallas kernels  31 us (95%)
  between operations  1.29 us (4%)
    pallas_call x1, Pallas kernels, shards(): pl.pallas_call(functools.partial(kernel, rows, cols), out_shape=(pltpu.VM...  29.7 us
    pallas_call x1, Pallas kernels, shards(): pl.pallas_call(store, out_shape=tuple((jax.ShapeDtypeStruct(v.shape, f32)...  1.34 us

profile of v6, /device:TPU:1, one launch (start us, length us, event | category | flops | bytes accessed | tf_op | source)
XLA Modules:
  0.0 32.3 jit_solution(2450701671972383475)
XLA Ops:
  1.3 29.7 %shard_map.94 = (f32[2,2,256,256]{3,2,1,0:T(8,128)S(1)}, f32[4,8,16,256]{3,2,1,0:T(8,128)S(1)}, f32[2,256,256]{2,1,0:T(8,128)S(1)}) custom-call(s32[2]{0:T(128)} %bitcast.11, s32[1]{0:T(128)} %bitcast.7.count_hbm, f32[2,2,256,256]{3,2,1,0:T(8,128)} %obj_hbm.1, f32[4,8,16,256]{3,2,1,0:T(8,128)} %bitcast.9, f32[2,256,256]{2,1,0:T(8,128)} %probe_hbm.1, ...), custom_call_target="tpu_custom_call" | custom-call | tf_op jit(solution)/shard_map/pallas_call | solution.py:632
  31.0 1.3 %shard_map.95 = (f32[2,2,256,256]{3,2,1,0:T(8,128)}, f32[4,8,16,256]{3,2,1,0:T(8,128)}, f32[2,256,256]{2,1,0:T(8,128)}) custom-call(f32[2,2,256,256]{3,2,1,0:T(8,128)S(1)} %get-tuple-element.9.obj, f32[4,8,16,256]{3,2,1,0:T(8,128)S(1)} %get-tuple-element.10.probe, f32[2,256,256]{2,1,0:T(8,128)S(1)} %get-tuple-element.11.part), custom_call_target="tpu_custom_call" | custom-call | tf_op jit(solution)/shard_map/pallas_call | solution.py:647
